TPU v7x, 256 devices: a whole 4x4x8 slice. The times are simulated.
256 devices in a mesh: seq: 8 (over z_lo, x), head: 32 (over z_hi, y, core).
Axes of the slice: x: 4, y: 4, z: 8 (z_hi: 4, z_lo: 2; z = z_hi * 2 + z_lo), core: 2. Of those that a mesh axis runs over, the one named last changes fastest.
Arguments:
- queries: bfloat16 [8192, 8192], P('seq', 'head'), may hold values from -8 to 8
- key_cols: bfloat16 [1024, 8192], P('head', 'seq'), may hold values from -8 to 8
- value_cols: bfloat16 [1024, 8192], P('head', 'seq'), may hold values from -6 to 6
- grad_out: bfloat16 [8192, 8192], P('seq', 'head'), may hold values from -6 to 6
- key_blocks: int32 [64, 24], replicated, may hold values from 0 to 63, as said below
- block_count: int32 [64], replicated, may hold values from 1 to 24
Outputs:
- attn_out: bfloat16 [8192, 8192], P('seq', 'head')
- grad_query: bfloat16 [8192, 8192], P('seq', 'head')
- grad_key_cols: bfloat16 [1024, 8192], P('head', 'seq')
- grad_value_cols: bfloat16 [1024, 8192], P('head', 'seq')
Inputs may be any that keep to these rules, and one draw needn't show every extreme that they name: `key_blocks`: in row a, the live entries are distinct key blocks not after a, in falling order, the first being a itself; entries after the live ones are ignored.
All inputs are finite; a program needn't handle non-finite values.
Results may differ from a plain program's by a relative error of at most 0.02.
Values may be sent and summed in bfloat16 or wider, within the bound.
No kernel may reach another device: no remote copies, remote signals or barrier semaphores. Data moves between devices by JAX's collectives and lax.ppermute only.
A program may use at most 128 MiB of HBM per device.

v0:
```python
import math

import jax
import jax.numpy as jnp
from jax import lax
from jax.sharding import PartitionSpec as P

DH = 128
HQ_DEV = 2
BLK = 128


def partner_2(value, axis, bit):
    return lax.ppermute(value, axis, [(i, i ^ 1 << bit) for i in range(lax.axis_size(axis))])


def block_pass(query_block, out_grad, key_tiles, value_tiles, tile_ids, tile_count, query_tile):
    block_rows = query_block.shape[0]
    head_dims = query_block.shape[2]
    slot_total = tile_ids.shape[0]
    scaling = 1.0 / math.sqrt(head_dims)
    key_pick = jnp.take(key_tiles, tile_ids, axis=1)
    value_pick = jnp.take(value_tiles, tile_ids, axis=1)
    scores = (
        jnp.einsum("thd,dnk->htnk", query_block, key_pick, preferred_element_type=jnp.float32)
        * scaling
    )
    query_pos = query_tile * block_rows + jnp.arange(block_rows, dtype=jnp.int32)
    key_pos = tile_ids[:, None] * block_rows + jnp.arange(block_rows, dtype=jnp.int32)[None, :]
    live_slot = jnp.arange(slot_total, dtype=jnp.int32) < tile_count
    allowed = live_slot[None, :, None] & (key_pos[None, :, :] <= query_pos[:, None, None])
    masked = jnp.where(allowed[None], scores, -1e30)
    row_top = jnp.max(masked, axis=(2, 3), keepdims=True)
    row_total = jnp.sum(
        jnp.where(allowed[None], jnp.exp(masked - row_top), 0.0), axis=(2, 3), keepdims=True
    )
    log_total = row_top + jnp.log(row_total)
    weights = jnp.where(allowed[None], jnp.exp(masked - log_total), 0.0)
    weights_low = weights.astype(jnp.bfloat16)
    attended = jnp.einsum(
        "htnk,dnk->thd", weights_low, value_pick, preferred_element_type=jnp.float32
    ).astype(jnp.bfloat16)
    row_dot = jnp.sum(out_grad.astype(jnp.float32) * attended.astype(jnp.float32), axis=2)
    grad_weights = jnp.einsum(
        "thd,dnk->htnk", out_grad, value_pick, preferred_element_type=jnp.float32
    )
    grad_scores = (
        weights * (grad_weights - jnp.transpose(row_dot)[:, :, None, None]) * scaling
    ).astype(jnp.bfloat16)
    grad_query = jnp.einsum(
        "htnk,dnk->thd", grad_scores, key_pick, preferred_element_type=jnp.float32
    ).astype(jnp.bfloat16)
    grad_keys = jnp.einsum(
        "htnk,thd->dnk", grad_scores, query_block, preferred_element_type=jnp.float32
    )
    grad_values = jnp.einsum(
        "htnk,thd->dnk", weights_low, out_grad, preferred_element_type=jnp.float32
    )
    return (attended, grad_query, grad_keys, grad_values)


def join_quarters(stacked, head_index):
    for bit_pos in (0, 1):
        partner = partner_2(stacked, "head", bit_pos)
        upper_side = head_index >> bit_pos & 1 == 1
        front_half = jnp.where(upper_side, partner, stacked)
        back_half = jnp.where(upper_side, stacked, partner)
        stacked = jnp.concatenate([front_half, back_half], axis=1)
    return stacked


def halve_rows(grad_terms, head_index):
    for bit_pos in (1, 0):
        half_rows = grad_terms.shape[1] // 2
        lower_half = grad_terms[:, :half_rows]
        upper_half = grad_terms[:, half_rows:]
        upper_side = head_index >> bit_pos & 1 == 1
        kept_half = jnp.where(upper_side, upper_half, lower_half)
        given_half = jnp.where(upper_side, lower_half, upper_half)
        grad_terms = kept_half + partner_2(given_half, "head", bit_pos)
    return grad_terms


def per_device(queries, key_cols, value_cols, grad_out, key_blocks, block_count):
    shard_rows = queries.shape[0]
    local_tiles = shard_rows // BLK
    seq_devices = lax.axis_size("seq")
    seq_index = lax.axis_index("seq")
    head_index = lax.axis_index("head")
    stacked = jnp.stack([key_cols, value_cols])
    gathered = lax.all_gather(stacked, "seq", axis=2, tiled=True)
    whole = join_quarters(gathered, head_index)
    tile_total = local_tiles * seq_devices
    key_tiles = whole[0].reshape(DH, tile_total, BLK)
    value_tiles = whole[1].reshape(DH, tile_total, BLK)
    first_tile = seq_index * local_tiles
    local_blocks = lax.dynamic_slice_in_dim(key_blocks, first_tile, local_tiles, 0)
    local_counts = lax.dynamic_slice_in_dim(block_count, first_tile, local_tiles, 0)
    per_step = 2
    step_count = local_tiles // per_step
    query_grid = queries.reshape(step_count, per_step, BLK, HQ_DEV, DH)
    grad_grid = grad_out.reshape(step_count, per_step, BLK, HQ_DEV, DH)
    slot_total = key_blocks.shape[1]
    block_grid = local_blocks.reshape(step_count, per_step, slot_total)
    count_grid = local_counts.reshape(step_count, per_step)
    tile_grid = (first_tile + jnp.arange(local_tiles, dtype=jnp.int32)).reshape(
        step_count, per_step
    )
    batched = jax.vmap(block_pass, in_axes=(0, 0, None, None, 0, 0, 0))

    def advance(running, inputs):
        key_sums, value_sums = running
        query_block, out_grad, tile_ids, tile_count, query_tile = inputs
        attended, grad_query, grad_keys, grad_values = batched(
            query_block, out_grad, key_tiles, value_tiles, tile_ids, tile_count, query_tile
        )
        flat_ids = tile_ids.reshape(-1)
        moved_keys = jnp.moveaxis(grad_keys, 0, 1).reshape(DH, per_step * slot_total, BLK)
        moved_values = jnp.moveaxis(grad_values, 0, 1).reshape(DH, per_step * slot_total, BLK)
        key_sums = key_sums.at[:, flat_ids, :].add(moved_keys)
        value_sums = value_sums.at[:, flat_ids, :].add(moved_values)
        return ((key_sums, value_sums), (attended, grad_query))

    zeros_sum = jnp.zeros((DH, tile_total, BLK), jnp.float32)
    (key_sums, value_sums), (attended, grad_query) = lax.scan(
        advance, (zeros_sum, zeros_sum), (query_grid, grad_grid, block_grid, count_grid, tile_grid)
    )
    attn_out = attended.reshape(shard_rows, HQ_DEV * DH)
    grad_q_out = grad_query.reshape(shard_rows, HQ_DEV * DH)
    grad_terms = jnp.stack(
        [key_sums.reshape(DH, tile_total * BLK), value_sums.reshape(DH, tile_total * BLK)]
    )
    owned = lax.psum_scatter(
        halve_rows(grad_terms, head_index), "seq", scatter_dimension=2, tiled=True
    )
    return (attn_out, grad_q_out, owned[0].astype(jnp.bfloat16), owned[1].astype(jnp.bfloat16))


def solution(mesh):
    placed = (P("seq", "head"), P("head", "seq"), P("head", "seq"), P("seq", "head"), P(), P())
    return jax.shard_map(
        per_device,
        mesh=mesh,
        in_specs=placed,
        out_specs=(P("seq", "head"), P("seq", "head"), P("head", "seq"), P("head", "seq")),
        check_vma=False,
    )
```

profile of v0, /device:TPU:8, one launch (start us, length us, event | category | flops | bytes accessed | tf_op | source)
XLA Modules:
  0.0 540.5 jit_solution(8212401329529801686)
XLA Ops:
  8.8 46.0 %all-gather.2.cloned.1.call-done = bf16[2,32,8192]{2,1,0:T(8,128)(2,1)} async-done(((bf16[2,32,1024]{2,1,0:T(8,128)(2,1)}), bf16[2,32,8192]{2,1,0:T(8,128)(2,1)}) %all-gather.2.cloned.1.call-update) | async-done | bytes 1048592 | tf_op jit(solution)/shard_map/all_gather | solution.py:91
  65.4 43.1 %collective-permute-done.1 = bf16[2,64,8192]{2,1,0:T(8,128)(2,1)} collective-permute-done((bf16[2,64,8192]{2,1,0:T(8,128)(2,1)}, bf16[2,64,8192]{2,1,0:T(8,128)(2,1)}, u32[]{:S(2)}, u32[]{:S(2)}) %collective-permute-start.1) | collective-permute-done | bytes 2097184 | tf_op jit(solution)/shard_map/ppermute | solution.py:14
  123.3 232.3 %while.16 = (s32[]{:T(128)}, f32[128,64,128]{2,0,1:T(8,128)}, f32[128,64,128]{2,0,1:T(8,128)}, bf16[4,2,128,2,128]{4,3,2,1,0:T(2,128)(2,1)}, bf16[4,2,128,2,128]...) while((s32[]{:T(128)}, f32[128,64,128]{2,0,1:T(8,128)}, ...), condition=%wide.region_6.8_spmd, body=%wide.region_0.7_spmd.sunk | while | flops 2463505408 | bytes 148587056 | solution.py:125
  135.4 3.5 gather_fusion.1
  140.1 5.9 %multiply_reduce_fusion.2 = (f32[2,128,2]{1,2,0:T(2,128)S(1)}, bf16[2,128,2,128]{1,3,2,0:T(8,128)(2,1)S(1)}) fusion(bf16[1,2,128,2,128]{4,3,2,1,0:T(2,128)(2,1)S(1)} %constant_dynamic-slice_fusion.10, f32[2,24,128,128,2]{3,2,4,1,0:T(8,128)} %copy-done.2, f32[2,2,128]{2,1,0:T(2,128)S(1)} %log_add_fusion.2, ...), kind=kOutput, calls=%fused_computation.32.clone.1 | convolution fusion | flops 411631104 | bytes 8917040 | tf_op jit(solution)/shard_map/while/body/eval_jaxpr/vmap(htnk,dnk->thd)/dot_general | solution.py:40
  152.4 6.1 %fusion.80 = f32[2,128,24,128,1]{3,1,4,2,0:T(8,128)} fusion(bf16[1,2,128,2,128]{4,3,2,1,0:T(2,128)(2,1)S(1)} %constant_dynamic-slice_fusion.10, f32[2,24,128,128,2]{3,2,4,1,0:T(8,128)} %copy-done.2, f32[2,2,128]{2,1,0:T(2,128)S(1)} %log_add_fusion.2, pred[2,128,24,128]{1,3,2,0:T(8,128)(4,1)S(1)} %compare_and_fusion.4), kind=kOutput, calls=%fused_computation.35.clone.1 | convolution fusion | flops 410517504 | bytes 10356736 | tf_op jit(solution)/shard_map/while/body/eval_jaxpr/vmap(htnk,thd->dnk)/dot_general | solution.py:56
  158.6 11.0 %scatter_fusion.1 = f32[128,64,128]{2,0,1:T(8,128)} fusion(f32[128,64,128]{2,0,1:T(8,128)} %get-tuple-element.244, s32[48]{0:T(128)S(1)} %fusion.74, f32[48,128,128]{2,1,0:T(8,128)} %bitcast.235), kind=kCustom, calls=%fused_computation.3.clone.1 | custom fusion | flops 786432 | bytes 9437376 | tf_op jit(solution)/shard_map/while/body/eval_jaxpr/scatter-add | solution.py:121
  172.6 10.1 %scatter_fusion = f32[128,64,128]{2,0,1:T(8,128)} fusion(f32[128,64,128]{2,0,1:T(8,128)} %get-tuple-element.243, s32[48]{0:T(128)S(1)} %fusion.74, f32[48,128,128]{2,1,0:T(8,128)S(1)} %bitcast.232), kind=kCustom, calls=%fused_computation.2.clone.1 | custom fusion | flops 786432 | bytes 9437376 | tf_op jit(solution)/shard_map/while/body/eval_jaxpr/scatter-add | solution.py:120
  194.8 3.5 gather_fusion.1
  199.5 5.9 %multiply_reduce_fusion.2 = (f32[2,128,2]{1,2,0:T(2,128)S(1)}, bf16[2,128,2,128]{1,3,2,0:T(8,128)(2,1)S(1)}) fusion(bf16[1,2,128,2,128]{4,3,2,1,0:T(2,128)(2,1)S(1)} %constant_dynamic-slice_fusion.10, f32[2,24,128,128,2]{3,2,4,1,0:T(8,128)} %copy-done.2, f32[2,2,128]{2,1,0:T(2,128)S(1)} %log_add_fusion.2, ...), kind=kOutput, calls=%fused_computation.32.clone.1 | convolution fusion | flops 411631104 | bytes 8917040 | tf_op jit(solution)/shard_map/while/body/eval_jaxpr/vmap(htnk,dnk->thd)/dot_general | solution.py:40
  211.8 6.1 %fusion.80 = f32[2,128,24,128,1]{3,1,4,2,0:T(8,128)} fusion(bf16[1,2,128,2,128]{4,3,2,1,0:T(2,128)(2,1)S(1)} %constant_dynamic-slice_fusion.10, f32[2,24,128,128,2]{3,2,4,1,0:T(8,128)} %copy-done.2, f32[2,2,128]{2,1,0:T(2,128)S(1)} %log_add_fusion.2, pred[2,128,24,128]{1,3,2,0:T(8,128)(4,1)S(1)} %compare_and_fusion.4), kind=kOutput, calls=%fused_computation.35.clone.1 | convolution fusion | flops 410517504 | bytes 10356736 | tf_op jit(solution)/shard_map/while/body/eval_jaxpr/vmap(htnk,thd->dnk)/dot_general | solution.py:56
  218.0 10.4 %scatter_fusion.1 = f32[128,64,128]{2,0,1:T(8,128)} fusion(f32[128,64,128]{2,0,1:T(8,128)} %get-tuple-element.244, s32[48]{0:T(128)S(1)} %fusion.74, f32[48,128,128]{2,1,0:T(8,128)} %bitcast.235), kind=kCustom, calls=%fused_computation.3.clone.1 | custom fusion | flops 786432 | bytes 9437376 | tf_op jit(solution)/shard_map/while/body/eval_jaxpr/scatter-add | solution.py:121
  231.5 9.4 %scatter_fusion = f32[128,64,128]{2,0,1:T(8,128)} fusion(f32[128,64,128]{2,0,1:T(8,128)} %get-tuple-element.243, s32[48]{0:T(128)S(1)} %fusion.74, f32[48,128,128]{2,1,0:T(8,128)S(1)} %bitcast.232), kind=kCustom, calls=%fused_computation.2.clone.1 | custom fusion | flops 786432 | bytes 9437376 | tf_op jit(solution)/shard_map/while/body/eval_jaxpr/scatter-add | solution.py:120
  257.6 5.9 %multiply_reduce_fusion.2 = (f32[2,128,2]{1,2,0:T(2,128)S(1)}, bf16[2,128,2,128]{1,3,2,0:T(8,128)(2,1)S(1)}) fusion(bf16[1,2,128,2,128]{4,3,2,1,0:T(2,128)(2,1)S(1)} %constant_dynamic-slice_fusion.10, f32[2,24,128,128,2]{3,2,4,1,0:T(8,128)} %copy-done.2, f32[2,2,128]{2,1,0:T(2,128)S(1)} %log_add_fusion.2, ...), kind=kOutput, calls=%fused_computation.32.clone.1 | convolution fusion | flops 411631104 | bytes 8917040 | tf_op jit(solution)/shard_map/while/body/eval_jaxpr/vmap(htnk,dnk->thd)/dot_general | solution.py:40
  270.0 6.1 %fusion.80 = f32[2,128,24,128,1]{3,1,4,2,0:T(8,128)} fusion(bf16[1,2,128,2,128]{4,3,2,1,0:T(2,128)(2,1)S(1)} %constant_dynamic-slice_fusion.10, f32[2,24,128,128,2]{3,2,4,1,0:T(8,128)} %copy-done.2, f32[2,2,128]{2,1,0:T(2,128)S(1)} %log_add_fusion.2, pred[2,128,24,128]{1,3,2,0:T(8,128)(4,1)S(1)} %compare_and_fusion.4), kind=kOutput, calls=%fused_computation.35.clone.1 | convolution fusion | flops 410517504 | bytes 10356736 | tf_op jit(solution)/shard_map/while/body/eval_jaxpr/vmap(htnk,thd->dnk)/dot_general | solution.py:56
  276.2 10.0 %scatter_fusion.1 = f32[128,64,128]{2,0,1:T(8,128)} fusion(f32[128,64,128]{2,0,1:T(8,128)} %get-tuple-element.244, s32[48]{0:T(128)S(1)} %fusion.74, f32[48,128,128]{2,1,0:T(8,128)} %bitcast.235), kind=kCustom, calls=%fused_computation.3.clone.1 | custom fusion | flops 786432 | bytes 9437376 | tf_op jit(solution)/shard_map/while/body/eval_jaxpr/scatter-add | solution.py:121
  289.2 9.1 %scatter_fusion = f32[128,64,128]{2,0,1:T(8,128)} fusion(f32[128,64,128]{2,0,1:T(8,128)} %get-tuple-element.243, s32[48]{0:T(128)S(1)} %fusion.74, f32[48,128,128]{2,1,0:T(8,128)S(1)} %bitcast.232), kind=kCustom, calls=%fused_computation.2.clone.1 | custom fusion | flops 786432 | bytes 9437376 | tf_op jit(solution)/shard_map/while/body/eval_jaxpr/scatter-add | solution.py:120
  310.3 3.5 gather_fusion.1
  315.1 5.9 %multiply_reduce_fusion.2 = (f32[2,128,2]{1,2,0:T(2,128)S(1)}, bf16[2,128,2,128]{1,3,2,0:T(8,128)(2,1)S(1)}) fusion(bf16[1,2,128,2,128]{4,3,2,1,0:T(2,128)(2,1)S(1)} %constant_dynamic-slice_fusion.10, f32[2,24,128,128,2]{3,2,4,1,0:T(8,128)} %copy-done.2, f32[2,2,128]{2,1,0:T(2,128)S(1)} %log_add_fusion.2, ...), kind=kOutput, calls=%fused_computation.32.clone.1 | convolution fusion | flops 411631104 | bytes 8917040 | tf_op jit(solution)/shard_map/while/body/eval_jaxpr/vmap(htnk,dnk->thd)/dot_general | solution.py:40
  327.4 6.1 %fusion.80 = f32[2,128,24,128,1]{3,1,4,2,0:T(8,128)} fusion(bf16[1,2,128,2,128]{4,3,2,1,0:T(2,128)(2,1)S(1)} %constant_dynamic-slice_fusion.10, f32[2,24,128,128,2]{3,2,4,1,0:T(8,128)} %copy-done.2, f32[2,2,128]{2,1,0:T(2,128)S(1)} %log_add_fusion.2, pred[2,128,24,128]{1,3,2,0:T(8,128)(4,1)S(1)} %compare_and_fusion.4), kind=kOutput, calls=%fused_computation.35.clone.1 | convolution fusion | flops 410517504 | bytes 10356736 | tf_op jit(solution)/shard_map/while/body/eval_jaxpr/vmap(htnk,thd->dnk)/dot_general | solution.py:56
  333.6 10.0 %scatter_fusion.1 = f32[128,64,128]{2,0,1:T(8,128)} fusion(f32[128,64,128]{2,0,1:T(8,128)} %get-tuple-element.244, s32[48]{0:T(128)S(1)} %fusion.74, f32[48,128,128]{2,1,0:T(8,128)} %bitcast.235), kind=kCustom, calls=%fused_computation.3.clone.1 | custom fusion | flops 786432 | bytes 9437376 | tf_op jit(solution)/shard_map/while/body/eval_jaxpr/scatter-add | solution.py:121
  346.6 9.0 %scatter_fusion = f32[128,64,128]{2,0,1:T(8,128)} fusion(f32[128,64,128]{2,0,1:T(8,128)} %get-tuple-element.243, s32[48]{0:T(128)S(1)} %fusion.74, f32[48,128,128]{2,1,0:T(8,128)S(1)} %bitcast.232), kind=kCustom, calls=%fused_computation.2.clone.1 | custom fusion | flops 786432 | bytes 9437376 | tf_op jit(solution)/shard_map/while/body/eval_jaxpr/scatter-add | solution.py:120
  355.6 6.6 %copy.44 = f32[128,64,128]{2,1,0:T(8,128)} copy(f32[128,64,128]{2,0,1:T(8,128)} %get-tuple-element.72) | data formatting | bytes 8388608 | tf_op jit(solution)/shard_map/while | solution.py:125
  362.2 4.9 stack_reshape.6
  367.2 4.7 constant_dynamic-update-slice_fusion.2
  371.9 4.4 copy.45
  376.2 5.0 stack_reshape.7
  381.2 4.6 constant_dynamic-update-slice_fusion.1
  385.8 4.0 slice_select_fusion
  390.5 91.2 %collective-permute-done.2 = f32[2,64,8192]{2,1,0:T(8,128)S(1)} collective-permute-done((f32[2,64,8192]{2,1,0:T(8,128)S(1)}, f32[2,64,8192]{2,1,0:T(8,128)S(1)}, u32[]{:S(2)}, u32[]{:S(2)}) %collective-permute-start.2) | collective-permute-done | bytes 4194336 | tf_op jit(solution)/shard_map/ppermute | solution.py:14
  482.7 4.1 collective-permute-done.3
  489.9 42.1 %reduce-scatter.2.cloned.1.call-done = f32[2,32,1024]{2,1,0:T(8,128)} async-done(((f32[2,32,8192]{2,1,0:T(8,128)}), f32[2,32,1024]{2,1,0:T(8,128)}) %reduce-scatter.2.cloned.1.call-update) | async-done | bytes 262160 | tf_op jit(solution)/shard_map/reduce_scatter | solution.py:133
  (190 shorter events, 127.2 us)
Async XLA Ops:
  7.2 53.9 %copy-start = (s32[64,24]{0,1:T(8,128)S(1)}, s32[64,24]{0,1:T(8,128)}, u32[]{:S(2)}) copy-start(s32[64,24]{0,1:T(8,128)} %param.14) | copy-start | bytes 18436
  7.2 47.7 %all-gather.2.cloned.1.call-start = ((), (), s32[]{:S(2)}) async-start(), calls=%async_computation.1 | async-start | bytes 1179648 | tf_op jit(solution)/shard_map/all_gather | solution.py:91
  8.8 523.2 %reduce-scatter.2.cloned.1.call-start = ((), (), s32[]{:S(2)}) async-start(), calls=%async_computation.2 | async-start | bytes 2359296 | tf_op jit(solution)/shard_map/reduce_scatter | solution.py:133
  54.8 2.9 collective-permute-start
  54.9 6.4 %copy-start.9 = (s32[64]{0:T(128)S(1)}, s32[64]{0:T(128)}, u32[]{:S(2)}) copy-start(s32[64]{0:T(128)} %param.15) | copy-start | bytes 772
  60.6 48.0 %collective-permute-start.1 = (bf16[2,64,8192]{2,1,0:T(8,128)(2,1)}, bf16[2,64,8192]{2,1,0:T(8,128)(2,1)}, u32[]{:S(2)}, u32[]{:S(2)}) collective-permute-start(bf16[2,64,8192]{2,1,0:T(8,128)(2,1)} %pad_maximum_fusion.1), channel_id=1, source_target_pairs={{0,2},{1,3},{2,0},{3,1},{4,6},{5,7},{6,4},{7,5},{8,10},{9,11},{10,... | collective-permute-start | bytes 6291464 | tf_op jit(solution)/shard_map/ppermute | solution.py:14
  130.8 2.7 copy-start.2
  138.9 7.1 %slice-start = ((s8[6291456]{0:T(1024)(128)(4,1)}), s8[4194304]{0:T(1024)(128)(4,1)S(1)}, s32[]{:S(2)}) async-start(s8[6291456]{0:T(1024)(128)(4,1)} %bitcast.233), calls=%async_computation.3 | async-start | bytes 8388608 | tf_op jit(solution)/shard_map/while
  140.1 5.9 %slice-start.1 = ((s8[6291456]{0:T(1024)(128)(4,1)}), s8[2097152]{0:T(1024)(128)(4,1)S(1)}, s32[]{:S(2)}) async-start(s8[6291456]{0:T(1024)(128)(4,1)} %bitcast.233), calls=%async_computation.4 | async-start | bytes 4194304 | tf_op jit(solution)/shard_map/while
  140.1 5.9 %copy-start.6 = (bf16[48,128,128]{2,1,0:T(8,128)(2,1)S(1)}, bf16[48,128,128]{2,1,0:T(8,128)(2,1)}, u32[]{:S(2)}) copy-start(bf16[48,128,128]{2,1,0:T(8,128)(2,1)} %gather_fusion.1) | copy-start | bytes 4718596 | tf_op jit(solution)/shard_map/while
  149.0 1.7 copy-start.4
  190.2 2.7 copy-start.2
  198.3 7.1 %slice-start = ((s8[6291456]{0:T(1024)(128)(4,1)}), s8[4194304]{0:T(1024)(128)(4,1)S(1)}, s32[]{:S(2)}) async-start(s8[6291456]{0:T(1024)(128)(4,1)} %bitcast.233), calls=%async_computation.3 | async-start | bytes 8388608 | tf_op jit(solution)/shard_map/while
  199.5 5.9 %slice-start.1 = ((s8[6291456]{0:T(1024)(128)(4,1)}), s8[2097152]{0:T(1024)(128)(4,1)S(1)}, s32[]{:S(2)}) async-start(s8[6291456]{0:T(1024)(128)(4,1)} %bitcast.233), calls=%async_computation.4 | async-start | bytes 4194304 | tf_op jit(solution)/shard_map/while
  199.5 5.9 %copy-start.6 = (bf16[48,128,128]{2,1,0:T(8,128)(2,1)S(1)}, bf16[48,128,128]{2,1,0:T(8,128)(2,1)}, u32[]{:S(2)}) copy-start(bf16[48,128,128]{2,1,0:T(8,128)(2,1)} %gather_fusion.1) | copy-start | bytes 4718596 | tf_op jit(solution)/shard_map/while
  208.4 1.7 copy-start.4
  248.3 2.7 copy-start.2
  256.5 7.1 %slice-start = ((s8[6291456]{0:T(1024)(128)(4,1)}), s8[4194304]{0:T(1024)(128)(4,1)S(1)}, s32[]{:S(2)}) async-start(s8[6291456]{0:T(1024)(128)(4,1)} %bitcast.233), calls=%async_computation.3 | async-start | bytes 8388608 | tf_op jit(solution)/shard_map/while
  257.6 5.9 %slice-start.1 = ((s8[6291456]{0:T(1024)(128)(4,1)}), s8[2097152]{0:T(1024)(128)(4,1)S(1)}, s32[]{:S(2)}) async-start(s8[6291456]{0:T(1024)(128)(4,1)} %bitcast.233), calls=%async_computation.4 | async-start | bytes 4194304 | tf_op jit(solution)/shard_map/while
  257.6 5.9 %copy-start.6 = (bf16[48,128,128]{2,1,0:T(8,128)(2,1)S(1)}, bf16[48,128,128]{2,1,0:T(8,128)(2,1)}, u32[]{:S(2)}) copy-start(bf16[48,128,128]{2,1,0:T(8,128)(2,1)} %gather_fusion.1) | copy-start | bytes 4718596 | tf_op jit(solution)/shard_map/while
  305.7 2.7 copy-start.2
  313.9 7.1 %slice-start = ((s8[6291456]{0:T(1024)(128)(4,1)}), s8[4194304]{0:T(1024)(128)(4,1)S(1)}, s32[]{:S(2)}) async-start(s8[6291456]{0:T(1024)(128)(4,1)} %bitcast.233), calls=%async_computation.3 | async-start | bytes 8388608 | tf_op jit(solution)/shard_map/while
  315.0 5.9 %slice-start.1 = ((s8[6291456]{0:T(1024)(128)(4,1)}), s8[2097152]{0:T(1024)(128)(4,1)S(1)}, s32[]{:S(2)}) async-start(s8[6291456]{0:T(1024)(128)(4,1)} %bitcast.233), calls=%async_computation.4 | async-start | bytes 4194304 | tf_op jit(solution)/shard_map/while
  315.1 5.9 %copy-start.6 = (bf16[48,128,128]{2,1,0:T(8,128)(2,1)S(1)}, bf16[48,128,128]{2,1,0:T(8,128)(2,1)}, u32[]{:S(2)}) copy-start(bf16[48,128,128]{2,1,0:T(8,128)(2,1)} %gather_fusion.1) | copy-start | bytes 4718596 | tf_op jit(solution)/shard_map/while
  324.0 1.7 copy-start.4
  367.2 4.7 copy-start.3
  385.8 95.9 %copy-start.5 = (f32[2,128,8192]{2,1,0:T(8,128)S(1)}, f32[2,128,8192]{2,1,0:T(8,128)}, u32[]{:S(2)}) copy-start(f32[2,128,8192]{2,1,0:T(8,128)} %constant_dynamic-update-slice_fusion.1) | copy-start | bytes 25165828
  389.8 91.9 %collective-permute-start.2 = (f32[2,64,8192]{2,1,0:T(8,128)S(1)}, f32[2,64,8192]{2,1,0:T(8,128)S(1)}, u32[]{:S(2)}, u32[]{:S(2)}) collective-permute-start(f32[2,64,8192]{2,1,0:T(8,128)S(1)} %slice_select_fusion), channel_id=1, source_target_pairs={{0,2},{1,3},{2,0},{3,1},{4,6},{5,7},{6,4},{7,5},{8,10},{9,11},{10,... | collective-permute-start | bytes 12582920 | tf_op jit(solution)/shard_map/ppermute | solution.py:14
  482.6 6.1 %copy-start.7 = (bf16[4,2,128,2,128]{4,3,2,1,0:T(2,128)(2,1)S(1)}, bf16[4,2,128,2,128]{4,3,2,1,0:T(2,128)(2,1)}, u32[]{:S(2)}) copy-start(bf16[4,2,128,2,128]{4,3,2,1,0:T(2,128)(2,1)} %get-tuple-element.70) | copy-start | bytes 1572868
  482.6 6.1 %copy-start.8 = (bf16[4,2,128,2,128]{4,3,2,1,0:T(2,128)(2,1)S(1)}, bf16[4,2,128,2,128]{4,3,2,1,0:T(2,128)(2,1)}, u32[]{:S(2)}) copy-start(bf16[4,2,128,2,128]{4,3,2,1,0:T(2,128)(2,1)} %get-tuple-element.71) | copy-start | bytes 1572868
  482.6 4.2 collective-permute-start.3
  486.9 46.8 %copy-start.1 = (s32[64,24]{0,1:T(8,128)S(1)}, s32[64,24]{0,1:T(8,128)}, u32[]{:S(2)}) copy-start(s32[64,24]{0,1:T(8,128)} %param.14) | copy-start | bytes 18436
  (1 other events, 1.7 us)
Sparse Core Ops, SparseCore 0:
  10.4 44.4 all-gather.1
  488.8 43.1 reduce-scatter.1
where the time goes:
time: 543 us; the launch traced here: 540 us
  waiting for transfers between devices  230 us (42%)
  other arithmetic  108 us (20%)
  local copies, waits for them, and re-layouts  103 us (19%)
  matrix products  84.3 us (16%)
  between operations  14.2 us (3%)
    ppermute x4, waiting for transfers between devices, partner_2(): lax.ppermute(value, axis, [(i, i ^ 1 << bit) for i in range(lax.axis_size...  141 us
    all_gather x1, waiting for transfers between devices, per_device(): gathered = lax.all_gather(stacked, 'seq', axis=2, tiled=True)  46 us
    reduce_scatter x1, waiting for transfers between devices, per_device(): lax.psum_scatter(halve_rows(grad_terms, head_index), 'seq', scatter_dimen...  42.1 us
    scatter-add x4, other arithmetic, advance(): value_sums = value_sums.at[:, flat_ids, :].add(moved_values)  41.4 us
    scatter-add x4, other arithmetic, advance(): key_sums = key_sums.at[:, flat_ids, :].add(moved_keys)  37.5 us
    dot_general x4, matrix products, block_pass(): jnp.einsum('htnk,thd->dnk', weights_low, out_grad, preferred_element_type...  24.5 us
    dot_general x4, matrix products, block_pass(): jnp.einsum('htnk,dnk->thd', weights_low, value_pick, preferred_element_ty...  23.6 us
    while x40, local copies, waits for them, and re-layouts  17.3 us
  transfers between devices with their start and end apart: 6, of which 6 were waited for; matrix products, arithmetic and copies ran while one was open for 1% of the time, Pallas kernels for 0%

commit v1 on v0

v1 whole, which is shorter than its diff:
```python
import math

import jax
import jax.numpy as jnp
from jax import lax
from jax.experimental import pallas as pl
from jax.experimental.pallas import tpu as pltpu
from jax.sharding import PartitionSpec as P

DH = 128
HQ_DEV = 2
BLK = 128
GRP = 4
QUARTER = 32
NEG = -1e30
SCALE = 1.0 / math.sqrt(DH)
LOG2E = 1.4426950408889634
NT = (((1,), (1,)), ((), ()))


def dot(left, right):
    return jnp.dot(left, right, preferred_element_type=jnp.float32)


def dot_nt(left, right):
    return lax.dot_general(left, right, NT, preferred_element_type=jnp.float32)


def attend_kernel(
    where_ref, blocks_ref, count_ref,
    q_ref, do_ref, ka_ref, kc_ref, va_ref, vb_ref, vc_ref, vd_ref,
    o_ref, dq_ref, k_keep, k_send, v_keep, v_send,
    kbuf, vbuf, dk, dv, scores, stage, in_sem, out_sem,
):
    seq = where_ref[0]
    quarter = where_ref[1]

    def rows_of(index):
        return pl.ds(pl.multiple_of(index * QUARTER, QUARTER), QUARTER)

    mine, other_y = rows_of(quarter), rows_of(quarter ^ 2)
    sib, sib_y = rows_of(quarter ^ 1), rows_of(quarter ^ 3)
    loads = []
    for src, dst in (
        (ka_ref.at[:, 0], kbuf.at[:, mine]),
        (ka_ref.at[:, 1], kbuf.at[:, other_y]),
        (kc_ref.at[:, 0], kbuf.at[:, sib]),
        (kc_ref.at[:, 1], kbuf.at[:, sib_y]),
        (va_ref, vbuf.at[:, mine]),
        (vb_ref, vbuf.at[:, other_y]),
        (vc_ref, vbuf.at[:, sib]),
        (vd_ref, vbuf.at[:, sib_y]),
    ):
        loads.append(pltpu.make_async_copy(src, dst, in_sem.at[len(loads)]))
    for load in loads:
        load.start()
    for shard in range(8):
        dk[shard] = jnp.zeros((DH, 1024), jnp.float32)
        dv[shard] = jnp.zeros((DH, 1024), jnp.float32)
    for load in loads:
        load.wait()

    def place(block):
        return block // 8, pl.ds(pl.multiple_of((block % 8) * BLK, BLK), BLK)

    def pick(buf, ids):
        parts = []
        for block in ids:
            shard, cols = place(block)
            parts.append(buf[shard, :, cols])
        return jnp.concatenate(parts, axis=1)

    def spread(buf, ids, total):
        for k, block in enumerate(ids):
            shard, cols = place(block)
            buf[shard, :, cols] += total[:, k * BLK : (k + 1) * BLK]

    def one_tile(i, carry):
        tile = seq * 8 + i
        live = count_ref[tile]
        rest = live - 1
        tail = rest % GRP
        full = rest // GRP
        rows = pl.ds(pl.multiple_of(i * BLK, BLK), BLK)
        q2 = q_ref[rows, :]
        do2 = do_ref[rows, :]
        q = jnp.concatenate([q2[:, :DH], q2[:, DH:]], axis=0)
        do = jnp.concatenate([do2[:, :DH], do2[:, DH:]], axis=0)

        def first_ids():
            return [tile] + [
                jnp.where(k <= tail, blocks_ref[tile, k], tile) for k in range(1, GRP)
            ]

        def later_ids(g):
            start = 1 + tail + GRP * (g - 1)
            return [blocks_ref[tile, start + k] for k in range(GRP)]

        ids0 = first_ids()
        s = dot(q, pick(kbuf, ids0))
        row = lax.broadcasted_iota(jnp.int32, (2 * BLK, BLK), 0) % BLK
        col = lax.broadcasted_iota(jnp.int32, (2 * BLK, BLK), 1)
        parts = [jnp.where(col <= row, s[:, :BLK], NEG)]
        for k in range(1, GRP):
            parts.append(jnp.where(k <= tail, s[:, k * BLK : (k + 1) * BLK], NEG))
        top = parts[0]
        for part in parts[1:]:
            top = jnp.maximum(top, part)
        scores[0] = jnp.concatenate(parts, axis=1)

        def fold_max(top, s):
            for k in range(GRP):
                top = jnp.maximum(top, s[:, k * BLK : (k + 1) * BLK])
            return top

        def pass_scores(g, top):
            s = dot(q, pick(kbuf, later_ids(g)))
            scores[g] = s
            return fold_max(top, s)

        top = lax.fori_loop(1, full + 1, pass_scores, top)
        peak = jnp.max(top, axis=1, keepdims=True) * (SCALE * LOG2E)

        def forward(g, ids, carry):
            total, out = carry
            p = jnp.exp2(scores[g] * (SCALE * LOG2E) - peak)
            for k in range(GRP):
                total = total + p[:, k * BLK : (k + 1) * BLK]
            out = out + dot_nt(p.astype(jnp.bfloat16), pick(vbuf, ids))
            return total, out

        zero = jnp.zeros((2 * BLK, BLK), jnp.float32)
        carry2 = forward(0, ids0, (zero, zero))
        total, out = lax.fori_loop(1, full + 1, lambda g, c: forward(g, later_ids(g), c), carry2)
        row_total = jnp.sum(total, axis=1, keepdims=True)
        attended = (out * (1.0 / row_total)).astype(jnp.bfloat16)
        o_ref[rows, :] = jnp.concatenate([attended[:BLK], attended[BLK:]], axis=1)
        log_total = peak + jnp.log2(row_total)
        row_dot = jnp.sum(
            do.astype(jnp.float32) * attended.astype(jnp.float32), axis=1, keepdims=True
        )
        q_t = jnp.transpose(q)
        do_t = jnp.transpose(do)

        def backward(g, ids, grad_q):
            w = jnp.exp2(scores[g] * (SCALE * LOG2E) - log_total)
            grad_w = dot(do, pick(vbuf, ids))
            grad_s = (w * (grad_w - row_dot)).astype(jnp.bfloat16)
            spread(dv, ids, dot(do_t, w.astype(jnp.bfloat16)))
            spread(dk, ids, dot(q_t, grad_s))
            return grad_q + dot_nt(grad_s, pick(kbuf, ids))

        grad_q = backward(0, ids0, zero)
        grad_q = lax.fori_loop(1, full + 1, lambda g, c: backward(g, later_ids(g), c), grad_q)
        grad_q = (grad_q * SCALE).astype(jnp.bfloat16)
        dq_ref[rows, :] = jnp.concatenate([grad_q[:BLK], grad_q[BLK:]], axis=1)
        return carry

    lax.fori_loop(0, 8, one_tile, 0)

    stores = []
    for shard in range(8):
        for buf, low, keep, send, scale in (
            (dk, stage.at[0], k_keep, k_send, SCALE),
            (dv, stage.at[1], v_keep, v_send, None),
        ):
            value = buf[shard]
            if scale is not None:
                value = value * scale
            low[shard] = value.astype(jnp.bfloat16)
            for rows, dst in (
                (mine, keep.at[shard, 0]),
                (other_y, keep.at[shard, 1]),
                (sib, send.at[shard, 0]),
                (sib_y, send.at[shard, 1]),
            ):
                copy = pltpu.make_async_copy(low.at[shard, rows], dst, out_sem.at[len(stores)])
                copy.start()
                stores.append(copy)
    for copy in stores:
        copy.wait()


def attend(where, key_blocks, block_count, queries, grad_out, parts):
    whole = pl.BlockSpec(memory_space=pltpu.VMEM)
    scalar = pl.BlockSpec(memory_space=pltpu.SMEM)
    away = pl.BlockSpec(memory_space=pl.ANY)
    half = jax.ShapeDtypeStruct((8, 2, QUARTER, 1024), jnp.bfloat16)
    grid_q = jax.ShapeDtypeStruct(queries.shape, jnp.bfloat16)
    return pl.pallas_call(
        attend_kernel,
        in_specs=[scalar] * 3 + [whole] * 2 + [away] * 6,
        out_specs=[whole] * 2 + [away] * 4,
        out_shape=[grid_q, grid_q, half, half, half, half],
        scratch_shapes=[
            pltpu.VMEM((8, DH, 1024), jnp.bfloat16),
            pltpu.VMEM((8, DH, 1024), jnp.bfloat16),
            pltpu.VMEM((8, DH, 1024), jnp.float32),
            pltpu.VMEM((8, DH, 1024), jnp.float32),
            pltpu.VMEM((6, 2 * BLK, GRP * BLK), jnp.float32),
            pltpu.VMEM((2, 8, DH, 1024), jnp.bfloat16),
            pltpu.SemaphoreType.DMA((8,)),
            pltpu.SemaphoreType.DMA((64,)),
        ],
        compiler_params=pltpu.CompilerParams(vmem_limit_bytes=48 << 20),
        name="attend",
    )(where, key_blocks, block_count, queries, grad_out, *parts)


def swap(value, bit):
    return lax.ppermute(value, "head", [(i, i ^ bit) for i in range(lax.axis_size("head"))])


def send_all(value):
    shards = lax.axis_size("seq")
    return lax.all_to_all(jnp.broadcast_to(value[None], (shards,) + value.shape), "seq", 0, 0)


def per_device(queries, key_cols, value_cols, grad_out, key_blocks, block_count):
    seq_index = lax.axis_index("seq")
    quarter = lax.axis_index("head") & 3
    upper = quarter >> 1 == 1

    v_mine = send_all(value_cols)
    k_pair = jnp.stack([key_cols, swap(key_cols, 2)])
    k_mine = send_all(k_pair)
    v_pair = swap(v_mine, 2)
    v_sib = swap(v_mine, 1)
    v_sib_pair = swap(v_pair, 1)
    k_sib = swap(k_mine, 1)

    where = jnp.stack([seq_index, quarter]).astype(jnp.int32)
    attn_out, grad_query, k_keep, k_send, v_keep, v_send = attend(
        where, key_blocks, block_count, queries, grad_out,
        (k_mine, k_sib, v_mine, v_pair, v_sib, v_sib_pair),
    )

    def add(left, right):
        return left.astype(jnp.float32) + right.astype(jnp.float32)

    v_half = add(v_keep, swap(v_send, 1)).astype(jnp.bfloat16)
    k_half = add(k_keep, swap(k_send, 1)).astype(jnp.bfloat16)
    v_quarter = add(v_half[:, 0], swap(v_half[:, 1], 2)).astype(jnp.bfloat16)
    k_got = lax.all_to_all(k_half, "seq", 0, 0)
    k_sum = jnp.sum(k_got.astype(jnp.float32), axis=0)
    v_got = lax.all_to_all(v_quarter, "seq", 0, 0)
    grad_value = jnp.sum(v_got.astype(jnp.float32), axis=0).astype(jnp.bfloat16)
    grad_key = (k_sum[0] + swap(k_sum[1], 2)).astype(jnp.bfloat16)
    return attn_out, grad_query, grad_key, grad_value


def solution(mesh):
    placed = (P("seq", "head"), P("head", "seq"), P("head", "seq"), P("seq", "head"), P(), P())
    return jax.shard_map(
        per_device,
        mesh=mesh,
        in_specs=placed,
        out_specs=(P("seq", "head"), P("seq", "head"), P("head", "seq"), P("head", "seq")),
        check_vma=False,
    )
```

time: 543 us -> 128 us (0.24)
  waiting for transfers between devices: 230 us -> 50.1 us
  other arithmetic: 108 us -> 4.43 us
  local copies, waits for them, and re-layouts: 103 us -> 3 us
  matrix products: 84.3 us -> 0 us
  starting transfers between devices: 1.34 us -> 49.9 us
  Pallas kernels: 0 us -> 20.2 us
  between operations: 14.2 us -> 0.73 us
    ppermute x4 -> x9, waiting for transfers between devices: 141 us -> 23.4 us  [swap(): lax.ppermute(value, 'head', [(i, i ^ bit) for i in range(lax.axis_size('h...]
    dot_general x24 -> x0, matrix products: 84.3 us -> none  [the longest x4 24.5 us: block_pass(): jnp.einsum('htnk,thd->dnk', weights_low, out_grad, preferred_element_type...]
    scatter-add x8 -> x0, other arithmetic: 78.9 us -> none  [the longest x4 41.4 us: advance(): value_sums = value_sums.at[:, flat_ids, :].add(moved_values)]
    all_to_all x0 -> x4, starting transfers between devices: none -> 47 us  [the longest x1 31.5 us: per_device(): k_got = lax.all_to_all(k_half, 'seq', 0, 0)]
    all_gather x1 -> x0, waiting for transfers between devices: 46 us -> none  [per_device(): gathered = lax.all_gather(stacked, 'seq', axis=2, tiled=True)]
    reduce_scatter x1 -> x0, waiting for transfers between devices: 42.1 us -> none  [per_device(): lax.psum_scatter(halve_rows(grad_terms, head_index), 'seq', scatter_dimen...]
    while x44 -> x0, local copies, waits for them, and re-layouts: 33.7 us -> none
    all_to_all x0 -> x4, waiting for transfers between devices: none -> 26.7 us  [the longest x2 18.7 us: send_all(): lax.all_to_all(jnp.broadcast_to(value[None], (shards,) + value.shape), 's...]
  transfers between devices with their start and end apart: 6 -> 13, of which waited for: 6 -> 9; matrix products, arithmetic and copies ran while one was open for 1% -> 3% of each run, Pallas kernels for 0% -> 0%
where the time goes in v1:
time: 128 us
  waiting for transfers between devices  50.1 us (39%)
  starting transfers between devices  49.9 us (39%)
  Pallas kernels  20.2 us (16%)
  other arithmetic  4.43 us (3%)
  local copies, waits for them, and re-layouts  3 us (2%)
    all_to_all x1, starting transfers between devices, per_device(): k_got = lax.all_to_all(k_half, 'seq', 0, 0)  31.5 us
    ppermute x9, waiting for transfers between devices, swap(): lax.ppermute(value, 'head', [(i, i ^ bit) for i in range(lax.axis_size('h...  23.4 us
    pallas_call x1, Pallas kernels, attend(): pl.pallas_call(attend_kernel, in_specs=[scalar] * 3 + [whole] * 2 + [away...  20.2 us
    all_to_all x2, waiting for transfers between devices, send_all(): lax.all_to_all(jnp.broadcast_to(value[None], (shards,) + value.shape), 's...  18.7 us
    all_to_all x2, starting transfers between devices, send_all(): lax.all_to_all(jnp.broadcast_to(value[None], (shards,) + value.shape), 's...  10.1 us
    all_to_all x1, waiting for transfers between devices, per_device(): v_got = lax.all_to_all(v_quarter, 'seq', 0, 0)  7.93 us
    all_to_all x1, starting transfers between devices, per_device(): v_got = lax.all_to_all(v_quarter, 'seq', 0, 0)  5.42 us
    ppermute x9, starting transfers between devices, swap(): lax.ppermute(value, 'head', [(i, i ^ bit) for i in range(lax.axis_size('h...  2.91 us
  transfers between devices with their start and end apart: 13, of which 9 were waited for; matrix products, arithmetic and copies ran while one was open for 3% of the time, Pallas kernels for 0%

profile of v1, /device:TPU:8, one launch (start us, length us, event | category | flops | bytes accessed | tf_op | source)
XLA Modules:
  0.0 128.3 jit_solution(7564261491930274185)
XLA Ops:
  0.6 1.7 %broadcast_in_dim.5 = bf16[8,32,1024]{2,1,0:T(8,128)(2,1)} broadcast(bf16[32,1024]{1,0:T(8,128)(2,1)} %param.8), dimensions={1,2} | broadcast | bytes 589824 | tf_op jit(solution)/shard_map/broadcast_in_dim | solution.py:216
  2.4 5.7 %all-to-all-start.1 = ((bf16[8,32,1024]{2,1,0:T(8,128)(2,1)}), bf16[8,32,1024]{2,1,0:T(8,128)(2,1)S(1)}, u32[]{:S(2)}, u32[]{:S(2)}) async-start(bf16[8,32,1024]{2,1,0:T(8,128)(2,1)} %broadcast_in_dim.5), calls=%async_computation.1 | async-start | bytes 1048576 | tf_op jit(solution)/shard_map/all_to_all | solution.py:216
  8.0 0.5 collective-permute-start
  8.6 3.8 %collective-permute-done = bf16[32,1024]{1,0:T(8,128)(2,1)S(1)} collective-permute-done((bf16[32,1024]{1,0:T(8,128)(2,1)S(1)}, bf16[32,1024]{1,0:T(8,128)(2,1)S(1)}, u32[]{:S(2)}, u32[]{:S(2)}) %collective-permute-start) | collective-permute-done | bytes 65568 | tf_op jit(solution)/shard_map/ppermute | solution.py:211
  12.4 5.2 %all-to-all-done.1.va_ref = bf16[8,32,1024]{2,1,0:T(8,128)(2,1)S(1)} async-done(((bf16[8,32,1024]{2,1,0:T(8,128)(2,1)}), bf16[8,32,1024]{2,1,0:T(8,128)(2,1)S(1)}, u32[]{:S(2)}, u32[]{:S(2)}) %all-to-all-start.1) | async-done | bytes 524320 | tf_op jit(solution)/shard_map/all_to_all | solution.py:216
  17.6 1.1 broadcast_in_dim.4
  18.7 4.4 %all-to-all-start = ((bf16[8,2,32,1024]{3,2,1,0:T(8,128)(2,1)}), bf16[8,2,32,1024]{3,2,1,0:T(8,128)(2,1)}, u32[]{:S(2)}, u32[]{:S(2)}) async-start(bf16[8,2,32,1024]{3,2,1,0:T(8,128)(2,1)} %broadcast_in_dim.4), calls=%async_computation | async-start | bytes 2097152 | tf_op jit(solution)/shard_map/all_to_all | solution.py:216
  23.1 0.5 collective-permute-start.2
  23.7 13.5 %all-to-all-done.ka_ref = bf16[8,2,32,1024]{3,2,1,0:T(8,128)(2,1)} async-done(((bf16[8,2,32,1024]{3,2,1,0:T(8,128)(2,1)}), bf16[8,2,32,1024]{3,2,1,0:T(8,128)(2,1)}, u32[]{:S(2)}, u32[]{:S(2)}) %all-to-all-start) | async-done | bytes 1048608 | tf_op jit(solution)/shard_map/all_to_all | solution.py:216
  37.2 0.5 collective-permute-start.3
  37.7 0.0 collective-permute-start.4
  37.7 0.1 copy.10.blocks_ref
  37.8 0.1 pad_add_fusion.where_ref
  37.9 2.4 %collective-permute-done.3.vc_ref = bf16[8,32,1024]{2,1,0:T(8,128)(2,1)S(1)} collective-permute-done((bf16[8,32,1024]{2,1,0:T(8,128)(2,1)S(1)}, bf16[8,32,1024]{2,1,0:T(8,128)(2,1)S(1)}, u32[]{:S(2)}, u32[]{:S(2)}) %collective-permute-start.3) | collective-permute-done | bytes 524320 | tf_op jit(solution)/shard_map/ppermute | solution.py:211
  40.2 1.1 collective-permute-done.4.vd_ref
  41.4 0.3 collective-permute-done.1.kc_ref
  41.7 20.2 %attend.1 = (bf16[1024,256]{1,0:T(8,128)(2,1)}, bf16[1024,256]{1,0:T(8,128)(2,1)}, bf16[8,2,32,1024]{3,2,1,0:T(8,128)(2,1)S(1)}, bf16[8,2,32,1024]{3,2,1,0:T(8,1...) custom-call(s32[2]{0:T(128)S(1)} %pad_add_fusion.where_ref, ...), custom_call_target="tpu_custom_call" | custom-call | tf_op jit(solution)/shard_map/attend/pallas_call | solution.py:190
  61.9 0.2 collective-permute-start.5
  62.1 0.4 collective-permute-start.7
  62.5 2.4 %collective-permute-done.5 = bf16[8,2,32,1024]{3,2,1,0:T(8,128)(2,1)S(1)} collective-permute-done((bf16[8,2,32,1024]{3,2,1,0:T(8,128)(2,1)S(1)}, bf16[8,2,32,1024]{3,2,1,0:T(8,128)(2,1)S(1)}, u32[]{:S(2)}, u32[]{:S(2)}) %collective-permute-start.5) | collective-permute-done | bytes 1048608 | tf_op jit(solution)/shard_map/ppermute | solution.py:211
  64.9 1.4 %add_convert_fusion.1 = bf16[8,2,32,1024]{3,2,1,0:T(8,128)(2,1)} fusion(bf16[8,2,32,1024]{3,2,1,0:T(8,128)(2,1)S(1)} %collective-permute-done.5, bf16[8,2,32,1024]{3,2,1,0:T(8,128)(2,1)S(1)} %get-tuple-element.12), kind=kLoop, calls=%fused_computation.2 | loop fusion | flops 2097152 | bytes 3145728 | tf_op jit(solution)/shard_map/convert_element_type | solution.py:242
  66.3 31.5 %all-to-all-start.2 = ((bf16[8,2,32,1024]{3,2,1,0:T(8,128)(2,1)}), bf16[8,2,32,1024]{3,2,1,0:T(8,128)(2,1)S(1)}, u32[]{:S(2)}, u32[]{:S(2)}) async-start(bf16[8,2,32,1024]{3,2,1,0:T(8,128)(2,1)} %add_convert_fusion.1), calls=%async_computation.2 | async-start | bytes 2097152 | tf_op jit(solution)/shard_map/all_to_all | solution.py:244
  97.8 0.4 add_convert_fusion
  98.2 0.3 collective-permute-start.8
  98.6 13.4 %collective-permute-done.8 = bf16[8,32,1024]{2,1,0:T(8,128)(2,1)S(1)} collective-permute-done((bf16[8,32,1024]{2,1,0:T(8,128)(2,1)S(1)}, bf16[8,32,1024]{2,1,0:T(8,128)(2,1)S(1)}, u32[]{:S(2)}, u32[]{:S(2)}) %collective-permute-start.8) | collective-permute-done | bytes 524320 | tf_op jit(solution)/shard_map/ppermute | solution.py:211
  112.0 1.0 fusion
  113.0 5.4 %all-to-all-start.3 = ((bf16[8,32,1024]{2,1,0:T(8,128)(2,1)}), bf16[8,32,1024]{2,1,0:T(8,128)(2,1)S(1)}, u32[]{:S(2)}, u32[]{:S(2)}) async-start(bf16[8,32,1024]{2,1,0:T(8,128)(2,1)} %fusion), calls=%async_computation.3 | async-start | bytes 1048576 | tf_op jit(solution)/shard_map/all_to_all | solution.py:246
  118.4 0.2 convert_reduce_fusion
  118.6 0.4 collective-permute-start.6
  119.0 7.9 %all-to-all-done.3 = bf16[8,32,1024]{2,1,0:T(8,128)(2,1)S(1)} async-done(((bf16[8,32,1024]{2,1,0:T(8,128)(2,1)}), bf16[8,32,1024]{2,1,0:T(8,128)(2,1)S(1)}, u32[]{:S(2)}, u32[]{:S(2)}) %all-to-all-start.3) | async-done | bytes 524320 | tf_op jit(solution)/shard_map/all_to_all | solution.py:246
  126.9 0.7 reduce_sum.22
  127.7 0.6 fusion.2
  (20 shorter events, 0.1 us)
Async XLA Ops:
  0.6 7.4 %copy-start.4 = (bf16[32,1024]{1,0:T(8,128)(2,1)S(1)}, bf16[32,1024]{1,0:T(8,128)(2,1)}, u32[]{:S(2)}) copy-start(bf16[32,1024]{1,0:T(8,128)(2,1)} %param.7) | copy-start | bytes 196612
  2.4 15.2 %all-to-all-start.1 = ((bf16[8,32,1024]{2,1,0:T(8,128)(2,1)}), bf16[8,32,1024]{2,1,0:T(8,128)(2,1)S(1)}, u32[]{:S(2)}, u32[]{:S(2)}) async-start(bf16[8,32,1024]{2,1,0:T(8,128)(2,1)} %broadcast_in_dim.5), calls=%async_computation.1 | async-start | bytes 1048576 | tf_op jit(solution)/shard_map/all_to_all | solution.py:216
  8.0 4.4 %collective-permute-start = (bf16[32,1024]{1,0:T(8,128)(2,1)S(1)}, bf16[32,1024]{1,0:T(8,128)(2,1)S(1)}, u32[]{:S(2)}, u32[]{:S(2)}) collective-permute-start(bf16[32,1024]{1,0:T(8,128)(2,1)S(1)} %copy-done.4), channel_id=1, source_target_pairs={{0,2},{1,3},{2,0},{3,1},{4,6},{5,7},{6,4},{7,5},{8,10},{9,11},{10,... | collective-permute-start | bytes 196616 | tf_op jit(solution)/shard_map/ppermute | solution.py:211
  18.7 19.0 %copy-start.5 = (s32[64,24]{0,1:T(8,128)S(1)}, s32[64,24]{0,1:T(8,128)}, u32[]{:S(2)}) copy-start(s32[64,24]{0,1:T(8,128)} %param.10) | copy-start | bytes 18436
  18.7 22.9 %copy-start = (bf16[1024,256]{1,0:T(8,128)(2,1)S(1)}, bf16[1024,256]{1,0:T(8,128)(2,1)}, u32[]{:S(2)}) copy-start(bf16[1024,256]{1,0:T(8,128)(2,1)} %q_ref.1) | copy-start | bytes 1572868
  18.7 22.9 %copy-start.1 = (bf16[1024,256]{1,0:T(8,128)(2,1)S(1)}, bf16[1024,256]{1,0:T(8,128)(2,1)}, u32[]{:S(2)}) copy-start(bf16[1024,256]{1,0:T(8,128)(2,1)} %do_ref.1) | copy-start | bytes 1572868
  18.7 22.9 %copy-start.2 = (s32[64]{0:T(128)S(1)}, s32[64]{0:T(128)}, u32[]{:S(2)}) copy-start(s32[64]{0:T(128)} %count_ref.1) | copy-start | bytes 772
  18.7 18.5 %all-to-all-start = ((bf16[8,2,32,1024]{3,2,1,0:T(8,128)(2,1)}), bf16[8,2,32,1024]{3,2,1,0:T(8,128)(2,1)}, u32[]{:S(2)}, u32[]{:S(2)}) async-start(bf16[8,2,32,1024]{3,2,1,0:T(8,128)(2,1)} %broadcast_in_dim.4), calls=%async_computation | async-start | bytes 2097152 | tf_op jit(solution)/shard_map/all_to_all | solution.py:216
  23.1 14.6 %collective-permute-start.2 = (bf16[8,32,1024]{2,1,0:T(8,128)(2,1)S(1)}, bf16[8,32,1024]{2,1,0:T(8,128)(2,1)S(1)}, u32[]{:S(2)}, u32[]{:S(2)}) collective-permute-start(bf16[8,32,1024]{2,1,0:T(8,128)(2,1)S(1)} %all-to-all-done.1.va_ref), channel_id=1, source_target_pairs={{0,2},{1,3},{2,0},{3,1},{4,6},{5,7},{6,4},{7,5},{8,10},{9,11},{10,... | collective-permute-start | bytes 1572872 | tf_op jit(solution)/shard_map/ppermute | solution.py:211
  37.2 4.5 %collective-permute-start.1 = (bf16[8,2,32,1024]{3,2,1,0:T(8,128)(2,1)}, bf16[8,2,32,1024]{3,2,1,0:T(8,128)(2,1)}, u32[]{:S(2)}, u32[]{:S(2)}) collective-permute-start(bf16[8,2,32,1024]{3,2,1,0:T(8,128)(2,1)} %all-to-all-done.ka_ref), channel_id=1, source_target_pairs={{0,1},{1,0},{2,3},{3,2},{4,5},{5,4},{6,7},{7,6},{8,9},{9,8},{10,11... | collective-permute-start | bytes 3145736 | tf_op jit(solution)/shard_map/ppermute | solution.py:211
  37.2 3.0 %collective-permute-start.3 = (bf16[8,32,1024]{2,1,0:T(8,128)(2,1)S(1)}, bf16[8,32,1024]{2,1,0:T(8,128)(2,1)S(1)}, u32[]{:S(2)}, u32[]{:S(2)}) collective-permute-start(bf16[8,32,1024]{2,1,0:T(8,128)(2,1)S(1)} %all-to-all-done.1.va_ref), channel_id=1, source_target_pairs={{0,1},{1,0},{2,3},{3,2},{4,5},{5,4},{6,7},{7,6},{8,9},{9,8},{10,11... | collective-permute-start | bytes 1572872 | tf_op jit(solution)/shard_map/ppermute | solution.py:211
  37.7 3.6 %collective-permute-start.4 = (bf16[8,32,1024]{2,1,0:T(8,128)(2,1)S(1)}, bf16[8,32,1024]{2,1,0:T(8,128)(2,1)S(1)}, u32[]{:S(2)}, u32[]{:S(2)}) collective-permute-start(bf16[8,32,1024]{2,1,0:T(8,128)(2,1)S(1)} %collective-permute-done.2.vb_ref), channel_id=1, source_target_pairs={{0,1},{1,0},{2,3},{3,2},{4,5},{5,4},{6,7},{7,6},{8,9},{9,8},{10,11... | collective-permute-start | bytes 1572872 | tf_op jit(solution)/shard_map/ppermute | solution.py:211
  61.9 3.0 %collective-permute-start.5 = (bf16[8,2,32,1024]{3,2,1,0:T(8,128)(2,1)S(1)}, bf16[8,2,32,1024]{3,2,1,0:T(8,128)(2,1)S(1)}, u32[]{:S(2)}, u32[]{:S(2)}) collective-permute-start(bf16[8,2,32,1024]{3,2,1,0:T(8,128)(2,1)S(1)} %get-tuple-element.13), channel_id=1, source_target_pairs={{0,1},{1,0},{2,3},{3,2},{4,5},{5,4},{6,7},{7,6},{8,9},{9,8},{10,11... | collective-permute-start | bytes 3145736 | tf_op jit(solution)/shard_map/ppermute | solution.py:211
  62.1 35.7 %collective-permute-start.7 = (bf16[8,2,32,1024]{3,2,1,0:T(8,128)(2,1)}, bf16[8,2,32,1024]{3,2,1,0:T(8,128)(2,1)S(1)}, u32[]{:S(2)}, u32[]{:S(2)}) collective-permute-start(bf16[8,2,32,1024]{3,2,1,0:T(8,128)(2,1)} %get-tuple-element.15), channel_id=1, source_target_pairs={{0,1},{1,0},{2,3},{3,2},{4,5},{5,4},{6,7},{7,6},{8,9},{9,8},{10,11... | collective-permute-start | bytes 3145736 | tf_op jit(solution)/shard_map/ppermute | solution.py:211
  66.3 31.5 %copy-start.3 = (bf16[8,2,32,1024]{3,2,1,0:T(8,128)(2,1)S(1)}, bf16[8,2,32,1024]{3,2,1,0:T(8,128)(2,1)}, u32[]{:S(2)}) copy-start(bf16[8,2,32,1024]{3,2,1,0:T(8,128)(2,1)} %get-tuple-element.14) | copy-start | bytes 3145732
  66.3 46.8 %all-to-all-start.2 = ((bf16[8,2,32,1024]{3,2,1,0:T(8,128)(2,1)}), bf16[8,2,32,1024]{3,2,1,0:T(8,128)(2,1)S(1)}, u32[]{:S(2)}, u32[]{:S(2)}) async-start(bf16[8,2,32,1024]{3,2,1,0:T(8,128)(2,1)} %add_convert_fusion.1), calls=%async_computation.2 | async-start | bytes 2097152 | tf_op jit(solution)/shard_map/all_to_all | solution.py:244
  98.2 13.8 %collective-permute-start.8 = (bf16[8,32,1024]{2,1,0:T(8,128)(2,1)S(1)}, bf16[8,32,1024]{2,1,0:T(8,128)(2,1)S(1)}, u32[]{:S(2)}, u32[]{:S(2)}) collective-permute-start(bf16[8,32,1024]{2,1,0:T(8,128)(2,1)S(1)} %slice_bitcast_fusion), channel_id=1, source_target_pairs={{0,2},{1,3},{2,0},{3,1},{4,6},{5,7},{6,4},{7,5},{8,10},{9,11},{10,... | collective-permute-start | bytes 1572872 | tf_op jit(solution)/shard_map/ppermute | solution.py:211
  113.0 13.9 %all-to-all-start.3 = ((bf16[8,32,1024]{2,1,0:T(8,128)(2,1)}), bf16[8,32,1024]{2,1,0:T(8,128)(2,1)S(1)}, u32[]{:S(2)}, u32[]{:S(2)}) async-start(bf16[8,32,1024]{2,1,0:T(8,128)(2,1)} %fusion), calls=%async_computation.3 | async-start | bytes 1048576 | tf_op jit(solution)/shard_map/all_to_all | solution.py:246
  118.6 9.0 %collective-permute-start.6 = (f32[32,1024]{1,0:T(8,128)S(1)}, f32[32,1024]{1,0:T(8,128)S(1)}, u32[]{:S(2)}, u32[]{:S(2)}) collective-permute-start(f32[32,1024]{1,0:T(8,128)S(1)} %slice_bitcast_fusion.2), channel_id=1, source_target_pairs={{0,2},{1,3},{2,0},{3,1},{4,6},{5,7},{6,4},{7,5},{8,10},{9,11},{10,... | collective-permute-start | bytes 393224 | tf_op jit(solution)/shard_map/ppermute | solution.py:211

commit v2 on v1

--- a/solution.py
+++ b/solution.py
@@ -11,6 +11,7 @@
 HQ_DEV = 2
 BLK = 128
 GRP = 4
+NNZ = 24
 QUARTER = 32
 NEG = -1e30
 SCALE = 1.0 / math.sqrt(DH)
@@ -24,6 +25,14 @@
 
 def dot_nt(left, right):
     return lax.dot_general(left, right, NT, preferred_element_type=jnp.float32)
+
+
+def wide(column):
+    return jnp.broadcast_to(column, (column.shape[0], BLK))
+
+
+def across(tile):
+    return jnp.concatenate([tile] * GRP, axis=1)
 
 
 def attend_kernel(
@@ -75,12 +84,9 @@
             shard, cols = place(block)
             buf[shard, :, cols] += total[:, k * BLK : (k + 1) * BLK]
 
-    def one_tile(i, carry):
+    def one_tile(i, later):
         tile = seq * 8 + i
-        live = count_ref[tile]
-        rest = live - 1
-        tail = rest % GRP
-        full = rest // GRP
+        tail = (count_ref[tile] - 1) % GRP
         rows = pl.ds(pl.multiple_of(i * BLK, BLK), BLK)
         q2 = q_ref[rows, :]
         do2 = do_ref[rows, :]
@@ -117,28 +123,30 @@
             s = dot(q, pick(kbuf, later_ids(g)))
             scores[g] = s
             return fold_max(top, s)
-
-        top = lax.fori_loop(1, full + 1, pass_scores, top)
-        peak = jnp.max(top, axis=1, keepdims=True) * (SCALE * LOG2E)
+        for g in range(1, later + 1):
+            top = pass_scores(g, top)
+        peak = wide(jnp.max(top, axis=1, keepdims=True) * (SCALE * LOG2E))
 
         def forward(g, ids, carry):
-            total, out = carry
-            p = jnp.exp2(scores[g] * (SCALE * LOG2E) - peak)
-            for k in range(GRP):
-                total = total + p[:, k * BLK : (k + 1) * BLK]
-            out = out + dot_nt(p.astype(jnp.bfloat16), pick(vbuf, ids))
-            return total, out
+            p = jnp.exp2(scores[g] * (SCALE * LOG2E) - across(peak))
+            values = jnp.concatenate(
+                [pick(vbuf, ids), jnp.ones((DH, GRP * BLK), jnp.bfloat16)], axis=0
+            )
+            return carry + dot_nt(p.astype(jnp.bfloat16), values)
 
         zero = jnp.zeros((2 * BLK, BLK), jnp.float32)
-        carry2 = forward(0, ids0, (zero, zero))
-        total, out = lax.fori_loop(1, full + 1, lambda g, c: forward(g, later_ids(g), c), carry2)
-        row_total = jnp.sum(total, axis=1, keepdims=True)
+        both = forward(0, ids0, jnp.zeros((2 * BLK, 2 * DH), jnp.float32))
+        for g in range(1, later + 1):
+            both = forward(g, later_ids(g), both)
+        out, row_total = both[:, :DH], both[:, DH:]
         attended = (out * (1.0 / row_total)).astype(jnp.bfloat16)
         o_ref[rows, :] = jnp.concatenate([attended[:BLK], attended[BLK:]], axis=1)
         log_total = peak + jnp.log2(row_total)
         row_dot = jnp.sum(
             do.astype(jnp.float32) * attended.astype(jnp.float32), axis=1, keepdims=True
         )
+        row_dot = across(wide(row_dot))
+        log_total = across(log_total)
         q_t = jnp.transpose(q)
         do_t = jnp.transpose(do)
 
@@ -151,12 +159,18 @@
             return grad_q + dot_nt(grad_s, pick(kbuf, ids))
 
         grad_q = backward(0, ids0, zero)
-        grad_q = lax.fori_loop(1, full + 1, lambda g, c: backward(g, later_ids(g), c), grad_q)
+        for g in range(1, later + 1):
+            grad_q = backward(g, later_ids(g), grad_q)
         grad_q = (grad_q * SCALE).astype(jnp.bfloat16)
         dq_ref[rows, :] = jnp.concatenate([grad_q[:BLK], grad_q[BLK:]], axis=1)
+
+    def any_tile(i, carry):
+        full = (count_ref[seq * 8 + i] - 1) // GRP
+        for v in range(NNZ // GRP):
+            pl.when(full == v)(lambda v=v: one_tile(i, v))
         return carry
 
-    lax.fori_loop(0, 8, one_tile, 0)
+    lax.fori_loop(0, 8, any_tile, 0)
 
     stores = []
     for shard in range(8):
@@ -197,7 +211,7 @@
             pltpu.VMEM((8, DH, 1024), jnp.bfloat16),
             pltpu.VMEM((8, DH, 1024), jnp.float32),
             pltpu.VMEM((8, DH, 1024), jnp.float32),
-            pltpu.VMEM((6, 2 * BLK, GRP * BLK), jnp.float32),
+            pltpu.VMEM((NNZ // GRP, 2 * BLK, GRP * BLK), jnp.float32),
             pltpu.VMEM((2, 8, DH, 1024), jnp.bfloat16),
             pltpu.SemaphoreType.DMA((8,)),
             pltpu.SemaphoreType.DMA((64,)),

time: 128 us -> 117 us (0.914)
  starting transfers between devices: 49.9 us -> 40 us
  Pallas kernels: 20.2 us -> 18 us
    all_to_all x1, starting transfers between devices: 31.5 us -> 21.6 us  [per_device(): k_got = lax.all_to_all(k_half, 'seq', 0, 0)]
    pallas_call x1, Pallas kernels: 20.2 us -> 18 us  [attend(): pl.pallas_call(attend_kernel, in_specs=[scalar] * 3 + [whole] * 2 + [away...]
where the time goes in v2:
time: 117 us; the launch traced here: 116 us
  waiting for transfers between devices  50.1 us (43%)
  starting transfers between devices  40 us (34%)
  Pallas kernels  18 us (15%)
  other arithmetic  4.43 us (4%)
  local copies, waits for them, and re-layouts  3 us (3%)
    ppermute x9, waiting for transfers between devices, swap(): lax.ppermute(value, 'head', [(i, i ^ bit) for i in range(lax.axis_size('h...  23.4 us
    all_to_all x1, starting transfers between devices, per_device(): k_got = lax.all_to_all(k_half, 'seq', 0, 0)  21.6 us
    all_to_all x2, waiting for transfers between devices, send_all(): lax.all_to_all(jnp.broadcast_to(value[None], (shards,) + value.shape), 's...  18.7 us
    pallas_call x1, Pallas kernels, attend(): pl.pallas_call(attend_kernel, in_specs=[scalar] * 3 + [whole] * 2 + [away...  18 us
    all_to_all x2, starting transfers between devices, send_all(): lax.all_to_all(jnp.broadcast_to(value[None], (shards,) + value.shape), 's...  10.1 us
    all_to_all x1, waiting for transfers between devices, per_device(): v_got = lax.all_to_all(v_quarter, 'seq', 0, 0)  7.93 us
    all_to_all x1, starting transfers between devices, per_device(): v_got = lax.all_to_all(v_quarter, 'seq', 0, 0)  5.42 us
    ppermute x9, starting transfers between devices, swap(): lax.ppermute(value, 'head', [(i, i ^ bit) for i in range(lax.axis_size('h...  2.91 us
  transfers between devices with their start and end apart: 13, of which 9 were waited for; matrix products, arithmetic and copies ran while one was open for 3% of the time, Pallas kernels for 0%

profile of v2, /device:TPU:8, one launch (start us, length us, event | category | flops | bytes accessed | tf_op | source)
XLA Modules:
  0.0 116.3 jit_solution(6050340123626292139)
XLA Ops:
  0.6 1.7 %broadcast_in_dim.5 = bf16[8,32,1024]{2,1,0:T(8,128)(2,1)} broadcast(bf16[32,1024]{1,0:T(8,128)(2,1)} %param.8), dimensions={1,2} | broadcast | bytes 589824 | tf_op jit(solution)/shard_map/broadcast_in_dim | solution.py:230
  2.4 5.7 %all-to-all-start.1 = ((bf16[8,32,1024]{2,1,0:T(8,128)(2,1)}), bf16[8,32,1024]{2,1,0:T(8,128)(2,1)S(1)}, u32[]{:S(2)}, u32[]{:S(2)}) async-start(bf16[8,32,1024]{2,1,0:T(8,128)(2,1)} %broadcast_in_dim.5), calls=%async_computation.1 | async-start | bytes 1048576 | tf_op jit(solution)/shard_map/all_to_all | solution.py:230
  8.0 0.5 collective-permute-start
  8.6 3.8 %collective-permute-done = bf16[32,1024]{1,0:T(8,128)(2,1)S(1)} collective-permute-done((bf16[32,1024]{1,0:T(8,128)(2,1)S(1)}, bf16[32,1024]{1,0:T(8,128)(2,1)S(1)}, u32[]{:S(2)}, u32[]{:S(2)}) %collective-permute-start) | collective-permute-done | bytes 65568 | tf_op jit(solution)/shard_map/ppermute | solution.py:225
  12.4 5.2 %all-to-all-done.1.va_ref = bf16[8,32,1024]{2,1,0:T(8,128)(2,1)S(1)} async-done(((bf16[8,32,1024]{2,1,0:T(8,128)(2,1)}), bf16[8,32,1024]{2,1,0:T(8,128)(2,1)S(1)}, u32[]{:S(2)}, u32[]{:S(2)}) %all-to-all-start.1) | async-done | bytes 524320 | tf_op jit(solution)/shard_map/all_to_all | solution.py:230
  17.6 1.1 broadcast_in_dim.4
  18.7 4.4 %all-to-all-start = ((bf16[8,2,32,1024]{3,2,1,0:T(8,128)(2,1)}), bf16[8,2,32,1024]{3,2,1,0:T(8,128)(2,1)}, u32[]{:S(2)}, u32[]{:S(2)}) async-start(bf16[8,2,32,1024]{3,2,1,0:T(8,128)(2,1)} %broadcast_in_dim.4), calls=%async_computation | async-start | bytes 2097152 | tf_op jit(solution)/shard_map/all_to_all | solution.py:230
  23.1 0.5 collective-permute-start.2
  23.7 13.5 %all-to-all-done.ka_ref = bf16[8,2,32,1024]{3,2,1,0:T(8,128)(2,1)} async-done(((bf16[8,2,32,1024]{3,2,1,0:T(8,128)(2,1)}), bf16[8,2,32,1024]{3,2,1,0:T(8,128)(2,1)}, u32[]{:S(2)}, u32[]{:S(2)}) %all-to-all-start) | async-done | bytes 1048608 | tf_op jit(solution)/shard_map/all_to_all | solution.py:230
  37.2 0.5 collective-permute-start.3
  37.7 0.0 collective-permute-start.4
  37.7 0.1 copy.10.blocks_ref
  37.8 0.1 pad_add_fusion.where_ref
  37.9 2.4 %collective-permute-done.3.vc_ref = bf16[8,32,1024]{2,1,0:T(8,128)(2,1)S(1)} collective-permute-done((bf16[8,32,1024]{2,1,0:T(8,128)(2,1)S(1)}, bf16[8,32,1024]{2,1,0:T(8,128)(2,1)S(1)}, u32[]{:S(2)}, u32[]{:S(2)}) %collective-permute-start.3) | collective-permute-done | bytes 524320 | tf_op jit(solution)/shard_map/ppermute | solution.py:225
  40.2 1.1 collective-permute-done.4.vd_ref
  41.4 0.3 collective-permute-done.1.kc_ref
  41.7 18.0 %attend.1 = (bf16[1024,256]{1,0:T(8,128)(2,1)}, bf16[1024,256]{1,0:T(8,128)(2,1)}, bf16[8,2,32,1024]{3,2,1,0:T(8,128)(2,1)S(1)}, bf16[8,2,32,1024]{3,2,1,0:T(8,1...) custom-call(s32[2]{0:T(128)S(1)} %pad_add_fusion.where_ref, ...), custom_call_target="tpu_custom_call" | custom-call | tf_op jit(solution)/shard_map/attend/pallas_call | solution.py:204
  59.7 0.2 collective-permute-start.5
  59.9 0.4 collective-permute-start.7
  60.3 2.4 %collective-permute-done.5 = bf16[8,2,32,1024]{3,2,1,0:T(8,128)(2,1)S(1)} collective-permute-done((bf16[8,2,32,1024]{3,2,1,0:T(8,128)(2,1)S(1)}, bf16[8,2,32,1024]{3,2,1,0:T(8,128)(2,1)S(1)}, u32[]{:S(2)}, u32[]{:S(2)}) %collective-permute-start.5) | collective-permute-done | bytes 1048608 | tf_op jit(solution)/shard_map/ppermute | solution.py:225
  62.7 1.4 %add_convert_fusion.1 = bf16[8,2,32,1024]{3,2,1,0:T(8,128)(2,1)} fusion(bf16[8,2,32,1024]{3,2,1,0:T(8,128)(2,1)S(1)} %collective-permute-done.5, bf16[8,2,32,1024]{3,2,1,0:T(8,128)(2,1)S(1)} %get-tuple-element.12), kind=kLoop, calls=%fused_computation.2 | loop fusion | flops 2097152 | bytes 3145728 | tf_op jit(solution)/shard_map/convert_element_type | solution.py:256
  64.1 21.6 %all-to-all-start.2 = ((bf16[8,2,32,1024]{3,2,1,0:T(8,128)(2,1)}), bf16[8,2,32,1024]{3,2,1,0:T(8,128)(2,1)S(1)}, u32[]{:S(2)}, u32[]{:S(2)}) async-start(bf16[8,2,32,1024]{3,2,1,0:T(8,128)(2,1)} %add_convert_fusion.1), calls=%async_computation.2 | async-start | bytes 2097152 | tf_op jit(solution)/shard_map/all_to_all | solution.py:258
  85.7 0.4 add_convert_fusion
  86.2 0.4 collective-permute-start.8
  86.5 13.4 %collective-permute-done.8 = bf16[8,32,1024]{2,1,0:T(8,128)(2,1)S(1)} collective-permute-done((bf16[8,32,1024]{2,1,0:T(8,128)(2,1)S(1)}, bf16[8,32,1024]{2,1,0:T(8,128)(2,1)S(1)}, u32[]{:S(2)}, u32[]{:S(2)}) %collective-permute-start.8) | collective-permute-done | bytes 524320 | tf_op jit(solution)/shard_map/ppermute | solution.py:225
  100.0 1.0 fusion
  101.0 5.4 %all-to-all-start.3 = ((bf16[8,32,1024]{2,1,0:T(8,128)(2,1)}), bf16[8,32,1024]{2,1,0:T(8,128)(2,1)S(1)}, u32[]{:S(2)}, u32[]{:S(2)}) async-start(bf16[8,32,1024]{2,1,0:T(8,128)(2,1)} %fusion), calls=%async_computation.3 | async-start | bytes 1048576 | tf_op jit(solution)/shard_map/all_to_all | solution.py:260
  106.4 0.2 convert_reduce_fusion
  106.6 0.4 collective-permute-start.6
  107.0 7.9 %all-to-all-done.3 = bf16[8,32,1024]{2,1,0:T(8,128)(2,1)S(1)} async-done(((bf16[8,32,1024]{2,1,0:T(8,128)(2,1)}), bf16[8,32,1024]{2,1,0:T(8,128)(2,1)S(1)}, u32[]{:S(2)}, u32[]{:S(2)}) %all-to-all-start.3) | async-done | bytes 524320 | tf_op jit(solution)/shard_map/all_to_all | solution.py:260
  114.9 0.7 reduce_sum.22
  115.6 0.6 fusion.2
  (20 shorter events, 0.1 us)
Async XLA Ops:
  0.6 7.4 %copy-start.4 = (bf16[32,1024]{1,0:T(8,128)(2,1)S(1)}, bf16[32,1024]{1,0:T(8,128)(2,1)}, u32[]{:S(2)}) copy-start(bf16[32,1024]{1,0:T(8,128)(2,1)} %param.7) | copy-start | bytes 196612
  2.4 15.2 %all-to-all-start.1 = ((bf16[8,32,1024]{2,1,0:T(8,128)(2,1)}), bf16[8,32,1024]{2,1,0:T(8,128)(2,1)S(1)}, u32[]{:S(2)}, u32[]{:S(2)}) async-start(bf16[8,32,1024]{2,1,0:T(8,128)(2,1)} %broadcast_in_dim.5), calls=%async_computation.1 | async-start | bytes 1048576 | tf_op jit(solution)/shard_map/all_to_all | solution.py:230
  8.0 4.4 %collective-permute-start = (bf16[32,1024]{1,0:T(8,128)(2,1)S(1)}, bf16[32,1024]{1,0:T(8,128)(2,1)S(1)}, u32[]{:S(2)}, u32[]{:S(2)}) collective-permute-start(bf16[32,1024]{1,0:T(8,128)(2,1)S(1)} %copy-done.4), channel_id=1, source_target_pairs={{0,2},{1,3},{2,0},{3,1},{4,6},{5,7},{6,4},{7,5},{8,10},{9,11},{10,... | collective-permute-start | bytes 196616 | tf_op jit(solution)/shard_map/ppermute | solution.py:225
  18.7 19.0 %copy-start.5 = (s32[64,24]{0,1:T(8,128)S(1)}, s32[64,24]{0,1:T(8,128)}, u32[]{:S(2)}) copy-start(s32[64,24]{0,1:T(8,128)} %param.10) | copy-start | bytes 18436
  18.7 22.9 %copy-start = (bf16[1024,256]{1,0:T(8,128)(2,1)S(1)}, bf16[1024,256]{1,0:T(8,128)(2,1)}, u32[]{:S(2)}) copy-start(bf16[1024,256]{1,0:T(8,128)(2,1)} %q_ref.1) | copy-start | bytes 1572868
  18.7 22.9 %copy-start.1 = (bf16[1024,256]{1,0:T(8,128)(2,1)S(1)}, bf16[1024,256]{1,0:T(8,128)(2,1)}, u32[]{:S(2)}) copy-start(bf16[1024,256]{1,0:T(8,128)(2,1)} %do_ref.1) | copy-start | bytes 1572868
  18.7 22.9 %copy-start.2 = (s32[64]{0:T(128)S(1)}, s32[64]{0:T(128)}, u32[]{:S(2)}) copy-start(s32[64]{0:T(128)} %count_ref.1) | copy-start | bytes 772
  18.7 18.5 %all-to-all-start = ((bf16[8,2,32,1024]{3,2,1,0:T(8,128)(2,1)}), bf16[8,2,32,1024]{3,2,1,0:T(8,128)(2,1)}, u32[]{:S(2)}, u32[]{:S(2)}) async-start(bf16[8,2,32,1024]{3,2,1,0:T(8,128)(2,1)} %broadcast_in_dim.4), calls=%async_computation | async-start | bytes 2097152 | tf_op jit(solution)/shard_map/all_to_all | solution.py:230
  23.1 14.6 %collective-permute-start.2 = (bf16[8,32,1024]{2,1,0:T(8,128)(2,1)S(1)}, bf16[8,32,1024]{2,1,0:T(8,128)(2,1)S(1)}, u32[]{:S(2)}, u32[]{:S(2)}) collective-permute-start(bf16[8,32,1024]{2,1,0:T(8,128)(2,1)S(1)} %all-to-all-done.1.va_ref), channel_id=1, source_target_pairs={{0,2},{1,3},{2,0},{3,1},{4,6},{5,7},{6,4},{7,5},{8,10},{9,11},{10,... | collective-permute-start | bytes 1572872 | tf_op jit(solution)/shard_map/ppermute | solution.py:225
  37.2 4.5 %collective-permute-start.1 = (bf16[8,2,32,1024]{3,2,1,0:T(8,128)(2,1)}, bf16[8,2,32,1024]{3,2,1,0:T(8,128)(2,1)}, u32[]{:S(2)}, u32[]{:S(2)}) collective-permute-start(bf16[8,2,32,1024]{3,2,1,0:T(8,128)(2,1)} %all-to-all-done.ka_ref), channel_id=1, source_target_pairs={{0,1},{1,0},{2,3},{3,2},{4,5},{5,4},{6,7},{7,6},{8,9},{9,8},{10,11... | collective-permute-start | bytes 3145736 | tf_op jit(solution)/shard_map/ppermute | solution.py:225
  37.2 3.0 %collective-permute-start.3 = (bf16[8,32,1024]{2,1,0:T(8,128)(2,1)S(1)}, bf16[8,32,1024]{2,1,0:T(8,128)(2,1)S(1)}, u32[]{:S(2)}, u32[]{:S(2)}) collective-permute-start(bf16[8,32,1024]{2,1,0:T(8,128)(2,1)S(1)} %all-to-all-done.1.va_ref), channel_id=1, source_target_pairs={{0,1},{1,0},{2,3},{3,2},{4,5},{5,4},{6,7},{7,6},{8,9},{9,8},{10,11... | collective-permute-start | bytes 1572872 | tf_op jit(solution)/shard_map/ppermute | solution.py:225
  37.7 3.6 %collective-permute-start.4 = (bf16[8,32,1024]{2,1,0:T(8,128)(2,1)S(1)}, bf16[8,32,1024]{2,1,0:T(8,128)(2,1)S(1)}, u32[]{:S(2)}, u32[]{:S(2)}) collective-permute-start(bf16[8,32,1024]{2,1,0:T(8,128)(2,1)S(1)} %collective-permute-done.2.vb_ref), channel_id=1, source_target_pairs={{0,1},{1,0},{2,3},{3,2},{4,5},{5,4},{6,7},{7,6},{8,9},{9,8},{10,11... | collective-permute-start | bytes 1572872 | tf_op jit(solution)/shard_map/ppermute | solution.py:225
  59.7 3.0 %collective-permute-start.5 = (bf16[8,2,32,1024]{3,2,1,0:T(8,128)(2,1)S(1)}, bf16[8,2,32,1024]{3,2,1,0:T(8,128)(2,1)S(1)}, u32[]{:S(2)}, u32[]{:S(2)}) collective-permute-start(bf16[8,2,32,1024]{3,2,1,0:T(8,128)(2,1)S(1)} %get-tuple-element.13), channel_id=1, source_target_pairs={{0,1},{1,0},{2,3},{3,2},{4,5},{5,4},{6,7},{7,6},{8,9},{9,8},{10,11... | collective-permute-start | bytes 3145736 | tf_op jit(solution)/shard_map/ppermute | solution.py:225
  59.9 25.8 %collective-permute-start.7 = (bf16[8,2,32,1024]{3,2,1,0:T(8,128)(2,1)}, bf16[8,2,32,1024]{3,2,1,0:T(8,128)(2,1)S(1)}, u32[]{:S(2)}, u32[]{:S(2)}) collective-permute-start(bf16[8,2,32,1024]{3,2,1,0:T(8,128)(2,1)} %get-tuple-element.15), channel_id=1, source_target_pairs={{0,1},{1,0},{2,3},{3,2},{4,5},{5,4},{6,7},{7,6},{8,9},{9,8},{10,11... | collective-permute-start | bytes 3145736 | tf_op jit(solution)/shard_map/ppermute | solution.py:225
  64.1 21.6 %copy-start.3 = (bf16[8,2,32,1024]{3,2,1,0:T(8,128)(2,1)S(1)}, bf16[8,2,32,1024]{3,2,1,0:T(8,128)(2,1)}, u32[]{:S(2)}) copy-start(bf16[8,2,32,1024]{3,2,1,0:T(8,128)(2,1)} %get-tuple-element.14) | copy-start | bytes 3145732
  64.1 36.9 %all-to-all-start.2 = ((bf16[8,2,32,1024]{3,2,1,0:T(8,128)(2,1)}), bf16[8,2,32,1024]{3,2,1,0:T(8,128)(2,1)S(1)}, u32[]{:S(2)}, u32[]{:S(2)}) async-start(bf16[8,2,32,1024]{3,2,1,0:T(8,128)(2,1)} %add_convert_fusion.1), calls=%async_computation.2 | async-start | bytes 2097152 | tf_op jit(solution)/shard_map/all_to_all | solution.py:258
  86.2 13.8 %collective-permute-start.8 = (bf16[8,32,1024]{2,1,0:T(8,128)(2,1)S(1)}, bf16[8,32,1024]{2,1,0:T(8,128)(2,1)S(1)}, u32[]{:S(2)}, u32[]{:S(2)}) collective-permute-start(bf16[8,32,1024]{2,1,0:T(8,128)(2,1)S(1)} %slice_bitcast_fusion), channel_id=1, source_target_pairs={{0,2},{1,3},{2,0},{3,1},{4,6},{5,7},{6,4},{7,5},{8,10},{9,11},{10,... | collective-permute-start | bytes 1572872 | tf_op jit(solution)/shard_map/ppermute | solution.py:225
  101.0 13.9 %all-to-all-start.3 = ((bf16[8,32,1024]{2,1,0:T(8,128)(2,1)}), bf16[8,32,1024]{2,1,0:T(8,128)(2,1)S(1)}, u32[]{:S(2)}, u32[]{:S(2)}) async-start(bf16[8,32,1024]{2,1,0:T(8,128)(2,1)} %fusion), calls=%async_computation.3 | async-start | bytes 1048576 | tf_op jit(solution)/shard_map/all_to_all | solution.py:260
  106.6 9.0 %collective-permute-start.6 = (f32[32,1024]{1,0:T(8,128)S(1)}, f32[32,1024]{1,0:T(8,128)S(1)}, u32[]{:S(2)}, u32[]{:S(2)}) collective-permute-start(f32[32,1024]{1,0:T(8,128)S(1)} %slice_bitcast_fusion.2), channel_id=1, source_target_pairs={{0,2},{1,3},{2,0},{3,1},{4,6},{5,7},{6,4},{7,5},{8,10},{9,11},{10,... | collective-permute-start | bytes 393224 | tf_op jit(solution)/shard_map/ppermute | solution.py:225

commit v3 on v2

--- a/solution.py
+++ b/solution.py
@@ -39,7 +39,7 @@
     where_ref, blocks_ref, count_ref,
     q_ref, do_ref, ka_ref, kc_ref, va_ref, vb_ref, vc_ref, vd_ref,
     o_ref, dq_ref, k_keep, k_send, v_keep, v_send,
-    kbuf, vbuf, dk, dv, scores, stage, in_sem, out_sem,
+    kbuf, vbuf, dk, dv, scores, grads, stage, in_sem, out_sem,
 ):
     seq = where_ref[0]
     quarter = where_ref[1]
@@ -129,6 +129,8 @@
 
         def forward(g, ids, carry):
             p = jnp.exp2(scores[g] * (SCALE * LOG2E) - across(peak))
+            scores[g] = p
+            grads[g] = dot(do, pick(vbuf, ids))
             values = jnp.concatenate(
                 [pick(vbuf, ids), jnp.ones((DH, GRP * BLK), jnp.bfloat16)], axis=0
             )
@@ -139,21 +141,20 @@
         for g in range(1, later + 1):
             both = forward(g, later_ids(g), both)
         out, row_total = both[:, :DH], both[:, DH:]
-        attended = (out * (1.0 / row_total)).astype(jnp.bfloat16)
+        share = 1.0 / row_total
+        attended = (out * share).astype(jnp.bfloat16)
         o_ref[rows, :] = jnp.concatenate([attended[:BLK], attended[BLK:]], axis=1)
-        log_total = peak + jnp.log2(row_total)
         row_dot = jnp.sum(
             do.astype(jnp.float32) * attended.astype(jnp.float32), axis=1, keepdims=True
         )
         row_dot = across(wide(row_dot))
-        log_total = across(log_total)
+        share = across(share)
         q_t = jnp.transpose(q)
         do_t = jnp.transpose(do)
 
         def backward(g, ids, grad_q):
-            w = jnp.exp2(scores[g] * (SCALE * LOG2E) - log_total)
-            grad_w = dot(do, pick(vbuf, ids))
-            grad_s = (w * (grad_w - row_dot)).astype(jnp.bfloat16)
+            w = scores[g] * share
+            grad_s = (w * (grads[g] - row_dot)).astype(jnp.bfloat16)
             spread(dv, ids, dot(do_t, w.astype(jnp.bfloat16)))
             spread(dk, ids, dot(q_t, grad_s))
             return grad_q + dot_nt(grad_s, pick(kbuf, ids))
@@ -212,6 +213,7 @@
             pltpu.VMEM((8, DH, 1024), jnp.float32),
             pltpu.VMEM((8, DH, 1024), jnp.float32),
             pltpu.VMEM((NNZ // GRP, 2 * BLK, GRP * BLK), jnp.float32),
+            pltpu.VMEM((NNZ // GRP, 2 * BLK, GRP * BLK), jnp.float32),
             pltpu.VMEM((2, 8, DH, 1024), jnp.bfloat16),
             pltpu.SemaphoreType.DMA((8,)),
             pltpu.SemaphoreType.DMA((64,)),

time: 117 us -> 112 us (0.957)
  starting transfers between devices: 40 us -> 35.4 us
    all_to_all x1, starting transfers between devices: 21.6 us -> 16.7 us  [per_device(): k_got = lax.all_to_all(k_half, 'seq', 0, 0)]
where the time goes in v3:
time: 112 us
  waiting for transfers between devices  49.7 us (44%)
  starting transfers between devices  35.4 us (32%)
  Pallas kernels  18.7 us (17%)
  other arithmetic  4.43 us (4%)
  local copies, waits for them, and re-layouts  3 us (3%)
    ppermute x9, waiting for transfers between devices, swap(): lax.ppermute(value, 'head', [(i, i ^ bit) for i in range(lax.axis_size('h...  23.2 us
    all_to_all x2, waiting for transfers between devices, send_all(): lax.all_to_all(jnp.broadcast_to(value[None], (shards,) + value.shape), 's...  18.7 us
    pallas_call x1, Pallas kernels, attend(): pl.pallas_call(attend_kernel, in_specs=[scalar] * 3 + [whole] * 2 + [away...  18.7 us
    all_to_all x1, starting transfers between devices, per_device(): k_got = lax.all_to_all(k_half, 'seq', 0, 0)  16.7 us
    all_to_all x2, starting transfers between devices, send_all(): lax.all_to_all(jnp.broadcast_to(value[None], (shards,) + value.shape), 's...  10.1 us
    all_to_all x1, waiting for transfers between devices, per_device(): v_got = lax.all_to_all(v_quarter, 'seq', 0, 0)  7.77 us
    all_to_all x1, starting transfers between devices, per_device(): v_got = lax.all_to_all(v_quarter, 'seq', 0, 0)  5.42 us
    ppermute x9, starting transfers between devices, swap(): lax.ppermute(value, 'head', [(i, i ^ bit) for i in range(lax.axis_size('h...  3.25 us
  transfers between devices with their start and end apart: 13, of which 9 were waited for; matrix products, arithmetic and copies ran while one was open for 3% of the time, Pallas kernels for 0%

profile of v3, /device:TPU:8, one launch (start us, length us, event | category | flops | bytes accessed | tf_op | source)
XLA Modules:
  0.0 112.0 jit_solution(1910760766154484559)
XLA Ops:
  0.6 1.7 %broadcast_in_dim.5 = bf16[8,32,1024]{2,1,0:T(8,128)(2,1)} broadcast(bf16[32,1024]{1,0:T(8,128)(2,1)} %param.8), dimensions={1,2} | broadcast | bytes 589824 | tf_op jit(solution)/shard_map/broadcast_in_dim | solution.py:232
  2.4 5.7 %all-to-all-start.1 = ((bf16[8,32,1024]{2,1,0:T(8,128)(2,1)}), bf16[8,32,1024]{2,1,0:T(8,128)(2,1)S(1)}, u32[]{:S(2)}, u32[]{:S(2)}) async-start(bf16[8,32,1024]{2,1,0:T(8,128)(2,1)} %broadcast_in_dim.5), calls=%async_computation.1 | async-start | bytes 1048576 | tf_op jit(solution)/shard_map/all_to_all | solution.py:232
  8.0 0.5 collective-permute-start
  8.6 3.8 %collective-permute-done = bf16[32,1024]{1,0:T(8,128)(2,1)S(1)} collective-permute-done((bf16[32,1024]{1,0:T(8,128)(2,1)S(1)}, bf16[32,1024]{1,0:T(8,128)(2,1)S(1)}, u32[]{:S(2)}, u32[]{:S(2)}) %collective-permute-start) | collective-permute-done | bytes 65568 | tf_op jit(solution)/shard_map/ppermute | solution.py:227
  12.4 5.2 %all-to-all-done.1.va_ref = bf16[8,32,1024]{2,1,0:T(8,128)(2,1)S(1)} async-done(((bf16[8,32,1024]{2,1,0:T(8,128)(2,1)}), bf16[8,32,1024]{2,1,0:T(8,128)(2,1)S(1)}, u32[]{:S(2)}, u32[]{:S(2)}) %all-to-all-start.1) | async-done | bytes 524320 | tf_op jit(solution)/shard_map/all_to_all | solution.py:232
  17.6 1.1 %broadcast_in_dim.4 = bf16[8,2,32,1024]{3,2,1,0:T(8,128)(2,1)} broadcast(bf16[2,32,1024]{2,1,0:T(8,128)(2,1)S(1)} %pad_maximum_fusion), dimensions={1,2,3} | broadcast | bytes 1179648 | tf_op jit(solution)/shard_map/broadcast_in_dim | solution.py:232
  18.7 4.4 %all-to-all-start = ((bf16[8,2,32,1024]{3,2,1,0:T(8,128)(2,1)}), bf16[8,2,32,1024]{3,2,1,0:T(8,128)(2,1)}, u32[]{:S(2)}, u32[]{:S(2)}) async-start(bf16[8,2,32,1024]{3,2,1,0:T(8,128)(2,1)} %broadcast_in_dim.4), calls=%async_computation | async-start | bytes 2097152 | tf_op jit(solution)/shard_map/all_to_all | solution.py:232
  23.1 0.5 collective-permute-start.2
  23.7 13.5 %all-to-all-done.ka_ref = bf16[8,2,32,1024]{3,2,1,0:T(8,128)(2,1)} async-done(((bf16[8,2,32,1024]{3,2,1,0:T(8,128)(2,1)}), bf16[8,2,32,1024]{3,2,1,0:T(8,128)(2,1)}, u32[]{:S(2)}, u32[]{:S(2)}) %all-to-all-start) | async-done | bytes 1048608 | tf_op jit(solution)/shard_map/all_to_all | solution.py:232
  37.2 0.5 collective-permute-start.3
  37.7 0.0 collective-permute-start.4
  37.7 0.1 copy.10.blocks_ref
  37.8 0.1 pad_add_fusion.where_ref
  37.9 2.4 %collective-permute-done.3.vc_ref = bf16[8,32,1024]{2,1,0:T(8,128)(2,1)S(1)} collective-permute-done((bf16[8,32,1024]{2,1,0:T(8,128)(2,1)S(1)}, bf16[8,32,1024]{2,1,0:T(8,128)(2,1)S(1)}, u32[]{:S(2)}, u32[]{:S(2)}) %collective-permute-start.3) | collective-permute-done | bytes 524320 | tf_op jit(solution)/shard_map/ppermute | solution.py:227
  40.2 1.1 collective-permute-done.4.vd_ref
  41.4 0.3 collective-permute-done.1.kc_ref
  41.7 18.7 %attend.1 = (bf16[1024,256]{1,0:T(8,128)(2,1)}, bf16[1024,256]{1,0:T(8,128)(2,1)}, bf16[8,2,32,1024]{3,2,1,0:T(8,128)(2,1)S(1)}, bf16[8,2,32,1024]{3,2,1,0:T(8,1...) custom-call(s32[2]{0:T(128)S(1)} %pad_add_fusion.where_ref, ...), custom_call_target="tpu_custom_call" | custom-call | tf_op jit(solution)/shard_map/attend/pallas_call | solution.py:205
  60.4 0.2 collective-permute-start.5
  60.6 0.4 collective-permute-start.7
  61.0 2.4 %collective-permute-done.5 = bf16[8,2,32,1024]{3,2,1,0:T(8,128)(2,1)S(1)} collective-permute-done((bf16[8,2,32,1024]{3,2,1,0:T(8,128)(2,1)S(1)}, bf16[8,2,32,1024]{3,2,1,0:T(8,128)(2,1)S(1)}, u32[]{:S(2)}, u32[]{:S(2)}) %collective-permute-start.5) | collective-permute-done | bytes 1048608 | tf_op jit(solution)/shard_map/ppermute | solution.py:227
  63.4 1.4 %add_convert_fusion.1 = bf16[8,2,32,1024]{3,2,1,0:T(8,128)(2,1)} fusion(bf16[8,2,32,1024]{3,2,1,0:T(8,128)(2,1)S(1)} %collective-permute-done.5, bf16[8,2,32,1024]{3,2,1,0:T(8,128)(2,1)S(1)} %get-tuple-element.12), kind=kLoop, calls=%fused_computation.2 | loop fusion | flops 2097152 | bytes 3145728 | tf_op jit(solution)/shard_map/convert_element_type | solution.py:258
  64.8 16.7 %all-to-all-start.2 = ((bf16[8,2,32,1024]{3,2,1,0:T(8,128)(2,1)}), bf16[8,2,32,1024]{3,2,1,0:T(8,128)(2,1)S(1)}, u32[]{:S(2)}, u32[]{:S(2)}) async-start(bf16[8,2,32,1024]{3,2,1,0:T(8,128)(2,1)} %add_convert_fusion.1), calls=%async_computation.2 | async-start | bytes 2097152 | tf_op jit(solution)/shard_map/all_to_all | solution.py:260
  81.5 0.4 add_convert_fusion
  81.9 0.5 collective-permute-start.8
  82.5 13.2 %collective-permute-done.8 = bf16[8,32,1024]{2,1,0:T(8,128)(2,1)S(1)} collective-permute-done((bf16[8,32,1024]{2,1,0:T(8,128)(2,1)S(1)}, bf16[8,32,1024]{2,1,0:T(8,128)(2,1)S(1)}, u32[]{:S(2)}, u32[]{:S(2)}) %collective-permute-start.8) | collective-permute-done | bytes 524320 | tf_op jit(solution)/shard_map/ppermute | solution.py:227
  95.7 1.0 fusion
  96.7 5.4 %all-to-all-start.3 = ((bf16[8,32,1024]{2,1,0:T(8,128)(2,1)}), bf16[8,32,1024]{2,1,0:T(8,128)(2,1)S(1)}, u32[]{:S(2)}, u32[]{:S(2)}) async-start(bf16[8,32,1024]{2,1,0:T(8,128)(2,1)} %fusion), calls=%async_computation.3 | async-start | bytes 1048576 | tf_op jit(solution)/shard_map/all_to_all | solution.py:262
  102.1 0.2 convert_reduce_fusion
  102.3 0.5 collective-permute-start.6
  102.9 7.8 %all-to-all-done.3 = bf16[8,32,1024]{2,1,0:T(8,128)(2,1)S(1)} async-done(((bf16[8,32,1024]{2,1,0:T(8,128)(2,1)}), bf16[8,32,1024]{2,1,0:T(8,128)(2,1)S(1)}, u32[]{:S(2)}, u32[]{:S(2)}) %all-to-all-start.3) | async-done | bytes 524320 | tf_op jit(solution)/shard_map/all_to_all | solution.py:262
  110.6 0.7 reduce_sum.22
  111.4 0.6 fusion.2
  (20 shorter events, 0.1 us)
Async XLA Ops:
  0.6 7.4 %copy-start.4 = (bf16[32,1024]{1,0:T(8,128)(2,1)S(1)}, bf16[32,1024]{1,0:T(8,128)(2,1)}, u32[]{:S(2)}) copy-start(bf16[32,1024]{1,0:T(8,128)(2,1)} %param.7) | copy-start | bytes 196612
  2.4 15.2 %all-to-all-start.1 = ((bf16[8,32,1024]{2,1,0:T(8,128)(2,1)}), bf16[8,32,1024]{2,1,0:T(8,128)(2,1)S(1)}, u32[]{:S(2)}, u32[]{:S(2)}) async-start(bf16[8,32,1024]{2,1,0:T(8,128)(2,1)} %broadcast_in_dim.5), calls=%async_computation.1 | async-start | bytes 1048576 | tf_op jit(solution)/shard_map/all_to_all | solution.py:232
  8.0 4.4 %collective-permute-start = (bf16[32,1024]{1,0:T(8,128)(2,1)S(1)}, bf16[32,1024]{1,0:T(8,128)(2,1)S(1)}, u32[]{:S(2)}, u32[]{:S(2)}) collective-permute-start(bf16[32,1024]{1,0:T(8,128)(2,1)S(1)} %copy-done.4), channel_id=1, source_target_pairs={{0,2},{1,3},{2,0},{3,1},{4,6},{5,7},{6,4},{7,5},{8,10},{9,11},{10,... | collective-permute-start | bytes 196616 | tf_op jit(solution)/shard_map/ppermute | solution.py:227
  18.7 19.0 %copy-start.5 = (s32[64,24]{0,1:T(8,128)S(1)}, s32[64,24]{0,1:T(8,128)}, u32[]{:S(2)}) copy-start(s32[64,24]{0,1:T(8,128)} %param.10) | copy-start | bytes 18436
  18.7 22.9 %copy-start = (bf16[1024,256]{1,0:T(8,128)(2,1)S(1)}, bf16[1024,256]{1,0:T(8,128)(2,1)}, u32[]{:S(2)}) copy-start(bf16[1024,256]{1,0:T(8,128)(2,1)} %q_ref.1) | copy-start | bytes 1572868
  18.7 22.9 %copy-start.1 = (bf16[1024,256]{1,0:T(8,128)(2,1)S(1)}, bf16[1024,256]{1,0:T(8,128)(2,1)}, u32[]{:S(2)}) copy-start(bf16[1024,256]{1,0:T(8,128)(2,1)} %do_ref.1) | copy-start | bytes 1572868
  18.7 22.9 %copy-start.2 = (s32[64]{0:T(128)S(1)}, s32[64]{0:T(128)}, u32[]{:S(2)}) copy-start(s32[64]{0:T(128)} %count_ref.1) | copy-start | bytes 772
  18.7 18.5 %all-to-all-start = ((bf16[8,2,32,1024]{3,2,1,0:T(8,128)(2,1)}), bf16[8,2,32,1024]{3,2,1,0:T(8,128)(2,1)}, u32[]{:S(2)}, u32[]{:S(2)}) async-start(bf16[8,2,32,1024]{3,2,1,0:T(8,128)(2,1)} %broadcast_in_dim.4), calls=%async_computation | async-start | bytes 2097152 | tf_op jit(solution)/shard_map/all_to_all | solution.py:232
  23.1 14.6 %collective-permute-start.2 = (bf16[8,32,1024]{2,1,0:T(8,128)(2,1)S(1)}, bf16[8,32,1024]{2,1,0:T(8,128)(2,1)S(1)}, u32[]{:S(2)}, u32[]{:S(2)}) collective-permute-start(bf16[8,32,1024]{2,1,0:T(8,128)(2,1)S(1)} %all-to-all-done.1.va_ref), channel_id=1, source_target_pairs={{0,2},{1,3},{2,0},{3,1},{4,6},{5,7},{6,4},{7,5},{8,10},{9,11},{10,... | collective-permute-start | bytes 1572872 | tf_op jit(solution)/shard_map/ppermute | solution.py:227
  37.2 4.5 %collective-permute-start.1 = (bf16[8,2,32,1024]{3,2,1,0:T(8,128)(2,1)}, bf16[8,2,32,1024]{3,2,1,0:T(8,128)(2,1)}, u32[]{:S(2)}, u32[]{:S(2)}) collective-permute-start(bf16[8,2,32,1024]{3,2,1,0:T(8,128)(2,1)} %all-to-all-done.ka_ref), channel_id=1, source_target_pairs={{0,1},{1,0},{2,3},{3,2},{4,5},{5,4},{6,7},{7,6},{8,9},{9,8},{10,11... | collective-permute-start | bytes 3145736 | tf_op jit(solution)/shard_map/ppermute | solution.py:227
  37.2 3.0 %collective-permute-start.3 = (bf16[8,32,1024]{2,1,0:T(8,128)(2,1)S(1)}, bf16[8,32,1024]{2,1,0:T(8,128)(2,1)S(1)}, u32[]{:S(2)}, u32[]{:S(2)}) collective-permute-start(bf16[8,32,1024]{2,1,0:T(8,128)(2,1)S(1)} %all-to-all-done.1.va_ref), channel_id=1, source_target_pairs={{0,1},{1,0},{2,3},{3,2},{4,5},{5,4},{6,7},{7,6},{8,9},{9,8},{10,11... | collective-permute-start | bytes 1572872 | tf_op jit(solution)/shard_map/ppermute | solution.py:227
  37.7 3.6 %collective-permute-start.4 = (bf16[8,32,1024]{2,1,0:T(8,128)(2,1)S(1)}, bf16[8,32,1024]{2,1,0:T(8,128)(2,1)S(1)}, u32[]{:S(2)}, u32[]{:S(2)}) collective-permute-start(bf16[8,32,1024]{2,1,0:T(8,128)(2,1)S(1)} %collective-permute-done.2.vb_ref), channel_id=1, source_target_pairs={{0,1},{1,0},{2,3},{3,2},{4,5},{5,4},{6,7},{7,6},{8,9},{9,8},{10,11... | collective-permute-start | bytes 1572872 | tf_op jit(solution)/shard_map/ppermute | solution.py:227
  60.4 3.0 %collective-permute-start.5 = (bf16[8,2,32,1024]{3,2,1,0:T(8,128)(2,1)S(1)}, bf16[8,2,32,1024]{3,2,1,0:T(8,128)(2,1)S(1)}, u32[]{:S(2)}, u32[]{:S(2)}) collective-permute-start(bf16[8,2,32,1024]{3,2,1,0:T(8,128)(2,1)S(1)} %get-tuple-element.13), channel_id=1, source_target_pairs={{0,1},{1,0},{2,3},{3,2},{4,5},{5,4},{6,7},{7,6},{8,9},{9,8},{10,11... | collective-permute-start | bytes 3145736 | tf_op jit(solution)/shard_map/ppermute | solution.py:227
  60.6 20.9 %collective-permute-start.7 = (bf16[8,2,32,1024]{3,2,1,0:T(8,128)(2,1)}, bf16[8,2,32,1024]{3,2,1,0:T(8,128)(2,1)S(1)}, u32[]{:S(2)}, u32[]{:S(2)}) collective-permute-start(bf16[8,2,32,1024]{3,2,1,0:T(8,128)(2,1)} %get-tuple-element.15), channel_id=1, source_target_pairs={{0,1},{1,0},{2,3},{3,2},{4,5},{5,4},{6,7},{7,6},{8,9},{9,8},{10,11... | collective-permute-start | bytes 3145736 | tf_op jit(solution)/shard_map/ppermute | solution.py:227
  64.8 16.7 %copy-start.3 = (bf16[8,2,32,1024]{3,2,1,0:T(8,128)(2,1)S(1)}, bf16[8,2,32,1024]{3,2,1,0:T(8,128)(2,1)}, u32[]{:S(2)}) copy-start(bf16[8,2,32,1024]{3,2,1,0:T(8,128)(2,1)} %get-tuple-element.14) | copy-start | bytes 3145732
  64.8 32.0 %all-to-all-start.2 = ((bf16[8,2,32,1024]{3,2,1,0:T(8,128)(2,1)}), bf16[8,2,32,1024]{3,2,1,0:T(8,128)(2,1)S(1)}, u32[]{:S(2)}, u32[]{:S(2)}) async-start(bf16[8,2,32,1024]{3,2,1,0:T(8,128)(2,1)} %add_convert_fusion.1), calls=%async_computation.2 | async-start | bytes 2097152 | tf_op jit(solution)/shard_map/all_to_all | solution.py:260
  81.9 13.8 %collective-permute-start.8 = (bf16[8,32,1024]{2,1,0:T(8,128)(2,1)S(1)}, bf16[8,32,1024]{2,1,0:T(8,128)(2,1)S(1)}, u32[]{:S(2)}, u32[]{:S(2)}) collective-permute-start(bf16[8,32,1024]{2,1,0:T(8,128)(2,1)S(1)} %slice_bitcast_fusion), channel_id=1, source_target_pairs={{0,2},{1,3},{2,0},{3,1},{4,6},{5,7},{6,4},{7,5},{8,10},{9,11},{10,... | collective-permute-start | bytes 1572872 | tf_op jit(solution)/shard_map/ppermute | solution.py:227
  96.7 13.9 %all-to-all-start.3 = ((bf16[8,32,1024]{2,1,0:T(8,128)(2,1)}), bf16[8,32,1024]{2,1,0:T(8,128)(2,1)S(1)}, u32[]{:S(2)}, u32[]{:S(2)}) async-start(bf16[8,32,1024]{2,1,0:T(8,128)(2,1)} %fusion), calls=%async_computation.3 | async-start | bytes 1048576 | tf_op jit(solution)/shard_map/all_to_all | solution.py:262
  102.3 9.0 %collective-permute-start.6 = (f32[32,1024]{1,0:T(8,128)S(1)}, f32[32,1024]{1,0:T(8,128)S(1)}, u32[]{:S(2)}, u32[]{:S(2)}) collective-permute-start(f32[32,1024]{1,0:T(8,128)S(1)} %slice_bitcast_fusion.2), channel_id=1, source_target_pairs={{0,2},{1,3},{2,0},{3,1},{4,6},{5,7},{6,4},{7,5},{8,10},{9,11},{10,... | collective-permute-start | bytes 393224 | tf_op jit(solution)/shard_map/ppermute | solution.py:227

commit v4 on v3

--- a/solution.py
+++ b/solution.py
@@ -260,8 +260,9 @@
     k_got = lax.all_to_all(k_half, "seq", 0, 0)
     k_sum = jnp.sum(k_got.astype(jnp.float32), axis=0)
     v_got = lax.all_to_all(v_quarter, "seq", 0, 0)
+    grad_key = (k_sum[0] + swap(k_sum[1], 2)).astype(jnp.bfloat16)
+    v_got, grad_key = lax.optimization_barrier((v_got, grad_key))
     grad_value = jnp.sum(v_got.astype(jnp.float32), axis=0).astype(jnp.bfloat16)
-    grad_key = (k_sum[0] + swap(k_sum[1], 2)).astype(jnp.bfloat16)
     return attn_out, grad_query, grad_key, grad_value
 
 

time: 112 us -> 111 us (level)
  Pallas kernels: 18.7 us -> 17.1 us
    all_to_all x1, waiting for transfers between devices: 7.77 us -> 2.6 us  [per_device(): v_got = lax.all_to_all(v_quarter, 'seq', 0, 0)]
    ppermute x9, waiting for transfers between devices: 23.2 us -> 27.7 us  [swap(): lax.ppermute(value, 'head', [(i, i ^ bit) for i in range(lax.axis_size('h...]
    pallas_call x1, Pallas kernels: 18.7 us -> 17.1 us  [attend(): pl.pallas_call(attend_kernel, in_specs=[scalar] * 3 + [whole] * 2 + [away...]
  transfers between devices with their start and end apart: 13 -> 13, of which waited for: 9 -> 10; matrix products, arithmetic and copies ran while one was open for 3% -> 3% of each run, Pallas kernels for 0% -> 0%
where the time goes in v4:
time: 111 us
  waiting for transfers between devices  49.1 us (44%)
  starting transfers between devices  36.2 us (33%)
  Pallas kernels  17.1 us (15%)
  other arithmetic  4.43 us (4%)
  local copies, waits for them, and re-layouts  3 us (3%)
    ppermute x9, waiting for transfers between devices, swap(): lax.ppermute(value, 'head', [(i, i ^ bit) for i in range(lax.axis_size('h...  27.7 us
    all_to_all x2, waiting for transfers between devices, send_all(): lax.all_to_all(jnp.broadcast_to(value[None], (shards,) + value.shape), 's...  18.7 us
    all_to_all x1, starting transfers between devices, per_device(): k_got = lax.all_to_all(k_half, 'seq', 0, 0)  17.5 us
    pallas_call x1, Pallas kernels, attend(): pl.pallas_call(attend_kernel, in_specs=[scalar] * 3 + [whole] * 2 + [away...  17.1 us
    all_to_all x2, starting transfers between devices, send_all(): lax.all_to_all(jnp.broadcast_to(value[None], (shards,) + value.shape), 's...  10.1 us
    all_to_all x1, starting transfers between devices, per_device(): v_got = lax.all_to_all(v_quarter, 'seq', 0, 0)  5.42 us
    ppermute x9, starting transfers between devices, swap(): lax.ppermute(value, 'head', [(i, i ^ bit) for i in range(lax.axis_size('h...  3.25 us
    broadcast_in_dim x2, local copies, waits for them, and re-layouts, send_all(): jnp.broadcast_to(value[None], (shards,) + value.shape)  2.85 us
  transfers between devices with their start and end apart: 13, of which 10 were waited for; matrix products, arithmetic and copies ran while one was open for 3% of the time, Pallas kernels for 0%

profile of v4, /device:TPU:8, one launch (start us, length us, event | category | flops | bytes accessed | tf_op | source)
XLA Modules:
  0.0 110.5 jit_solution(14857107741803428279)
XLA Ops:
  0.6 1.7 %broadcast_in_dim.5 = bf16[8,32,1024]{2,1,0:T(8,128)(2,1)} broadcast(bf16[32,1024]{1,0:T(8,128)(2,1)} %param.8), dimensions={1,2} | broadcast | bytes 589824 | tf_op jit(solution)/shard_map/broadcast_in_dim | solution.py:232
  2.4 5.7 %all-to-all-start.1 = ((bf16[8,32,1024]{2,1,0:T(8,128)(2,1)}), bf16[8,32,1024]{2,1,0:T(8,128)(2,1)S(1)}, u32[]{:S(2)}, u32[]{:S(2)}) async-start(bf16[8,32,1024]{2,1,0:T(8,128)(2,1)} %broadcast_in_dim.5), calls=%async_computation.1 | async-start | bytes 1048576 | tf_op jit(solution)/shard_map/all_to_all | solution.py:232
  8.0 0.5 collective-permute-start
  8.6 3.8 %collective-permute-done = bf16[32,1024]{1,0:T(8,128)(2,1)S(1)} collective-permute-done((bf16[32,1024]{1,0:T(8,128)(2,1)S(1)}, bf16[32,1024]{1,0:T(8,128)(2,1)S(1)}, u32[]{:S(2)}, u32[]{:S(2)}) %collective-permute-start) | collective-permute-done | bytes 65568 | tf_op jit(solution)/shard_map/ppermute | solution.py:227
  12.4 5.2 %all-to-all-done.1.va_ref = bf16[8,32,1024]{2,1,0:T(8,128)(2,1)S(1)} async-done(((bf16[8,32,1024]{2,1,0:T(8,128)(2,1)}), bf16[8,32,1024]{2,1,0:T(8,128)(2,1)S(1)}, u32[]{:S(2)}, u32[]{:S(2)}) %all-to-all-start.1) | async-done | bytes 524320 | tf_op jit(solution)/shard_map/all_to_all | solution.py:232
  17.6 1.1 %broadcast_in_dim.4 = bf16[8,2,32,1024]{3,2,1,0:T(8,128)(2,1)} broadcast(bf16[2,32,1024]{2,1,0:T(8,128)(2,1)S(1)} %pad_maximum_fusion), dimensions={1,2,3} | broadcast | bytes 1179648 | tf_op jit(solution)/shard_map/broadcast_in_dim | solution.py:232
  18.7 4.4 %all-to-all-start = ((bf16[8,2,32,1024]{3,2,1,0:T(8,128)(2,1)}), bf16[8,2,32,1024]{3,2,1,0:T(8,128)(2,1)}, u32[]{:S(2)}, u32[]{:S(2)}) async-start(bf16[8,2,32,1024]{3,2,1,0:T(8,128)(2,1)} %broadcast_in_dim.4), calls=%async_computation | async-start | bytes 2097152 | tf_op jit(solution)/shard_map/all_to_all | solution.py:232
  23.1 0.5 collective-permute-start.2
  23.7 13.5 %all-to-all-done.ka_ref = bf16[8,2,32,1024]{3,2,1,0:T(8,128)(2,1)} async-done(((bf16[8,2,32,1024]{3,2,1,0:T(8,128)(2,1)}), bf16[8,2,32,1024]{3,2,1,0:T(8,128)(2,1)}, u32[]{:S(2)}, u32[]{:S(2)}) %all-to-all-start) | async-done | bytes 1048608 | tf_op jit(solution)/shard_map/all_to_all | solution.py:232
  37.2 0.5 collective-permute-start.3
  37.7 0.1 copy.10.blocks_ref
  37.8 0.1 pad_add_fusion.where_ref
  37.9 2.4 %collective-permute-done.3.vc_ref = bf16[8,32,1024]{2,1,0:T(8,128)(2,1)S(1)} collective-permute-done((bf16[8,32,1024]{2,1,0:T(8,128)(2,1)S(1)}, bf16[8,32,1024]{2,1,0:T(8,128)(2,1)S(1)}, u32[]{:S(2)}, u32[]{:S(2)}) %collective-permute-start.3) | collective-permute-done | bytes 524320 | tf_op jit(solution)/shard_map/ppermute | solution.py:227
  40.2 1.1 %collective-permute-done.4.vd_ref = bf16[8,32,1024]{2,1,0:T(8,128)(2,1)S(1)} collective-permute-done((bf16[8,32,1024]{2,1,0:T(8,128)(2,1)S(1)}, bf16[8,32,1024]{2,1,0:T(8,128)(2,1)S(1)}, u32[]{:S(2)}, u32[]{:S(2)}) %collective-permute-start.4) | collective-permute-done | bytes 524320 | tf_op jit(solution)/shard_map/ppermute | solution.py:227
  41.4 0.3 collective-permute-done.1.kc_ref
  41.7 17.1 %attend.1 = (bf16[1024,256]{1,0:T(8,128)(2,1)}, bf16[1024,256]{1,0:T(8,128)(2,1)}, bf16[8,2,32,1024]{3,2,1,0:T(8,128)(2,1)S(1)}, bf16[8,2,32,1024]{3,2,1,0:T(8,1...) custom-call(s32[2]{0:T(128)S(1)} %pad_add_fusion.where_ref, ...), custom_call_target="tpu_custom_call" | custom-call | tf_op jit(solution)/shard_map/attend/pallas_call | solution.py:205
  58.8 0.2 collective-permute-start.7
  59.0 0.4 collective-permute-start.5
  59.4 2.4 %collective-permute-done.7 = bf16[8,2,32,1024]{3,2,1,0:T(8,128)(2,1)S(1)} collective-permute-done((bf16[8,2,32,1024]{3,2,1,0:T(8,128)(2,1)S(1)}, bf16[8,2,32,1024]{3,2,1,0:T(8,128)(2,1)S(1)}, u32[]{:S(2)}, u32[]{:S(2)}) %collective-permute-start.7) | collective-permute-done | bytes 1048608 | tf_op jit(solution)/shard_map/ppermute | solution.py:227
  61.8 1.4 %add_convert_fusion = bf16[8,2,32,1024]{3,2,1,0:T(8,128)(2,1)} fusion(bf16[8,2,32,1024]{3,2,1,0:T(8,128)(2,1)S(1)} %collective-permute-done.7, bf16[8,2,32,1024]{3,2,1,0:T(8,128)(2,1)S(1)} %get-tuple-element.16), kind=kLoop, calls=%fused_computation.1 | loop fusion | flops 2097152 | bytes 3145728 | tf_op jit(solution)/shard_map/convert_element_type | solution.py:258
  63.2 17.5 %all-to-all-start.3 = ((bf16[8,2,32,1024]{3,2,1,0:T(8,128)(2,1)}), bf16[8,2,32,1024]{3,2,1,0:T(8,128)(2,1)S(1)}, u32[]{:S(2)}, u32[]{:S(2)}) async-start(bf16[8,2,32,1024]{3,2,1,0:T(8,128)(2,1)} %add_convert_fusion), calls=%async_computation.3 | async-start | bytes 2097152 | tf_op jit(solution)/shard_map/all_to_all | solution.py:260
  80.7 0.4 add_convert_fusion.1
  81.1 0.5 collective-permute-start.6
  81.6 13.2 %collective-permute-done.6 = bf16[8,32,1024]{2,1,0:T(8,128)(2,1)S(1)} collective-permute-done((bf16[8,32,1024]{2,1,0:T(8,128)(2,1)S(1)}, bf16[8,32,1024]{2,1,0:T(8,128)(2,1)S(1)}, u32[]{:S(2)}, u32[]{:S(2)}) %collective-permute-start.6) | collective-permute-done | bytes 524320 | tf_op jit(solution)/shard_map/ppermute | solution.py:227
  94.9 1.0 fusion
  95.9 5.4 %all-to-all-start.2 = ((bf16[8,32,1024]{2,1,0:T(8,128)(2,1)}), bf16[8,32,1024]{2,1,0:T(8,128)(2,1)S(1)}, u32[]{:S(2)}, u32[]{:S(2)}) async-start(bf16[8,32,1024]{2,1,0:T(8,128)(2,1)} %fusion), calls=%async_computation.2 | async-start | bytes 1048576 | tf_op jit(solution)/shard_map/all_to_all | solution.py:262
  101.3 0.2 convert_reduce_fusion
  101.5 0.5 collective-permute-start.8
  102.1 4.5 %collective-permute-done.8 = f32[32,1024]{1,0:T(8,128)S(1)} collective-permute-done((f32[32,1024]{1,0:T(8,128)S(1)}, f32[32,1024]{1,0:T(8,128)S(1)}, u32[]{:S(2)}, u32[]{:S(2)}) %collective-permute-start.8) | collective-permute-done | bytes 131104 | tf_op jit(solution)/shard_map/ppermute | solution.py:227
  106.6 0.6 fusion.2
  107.2 2.6 %all-to-all-done.2 = bf16[8,32,1024]{2,1,0:T(8,128)(2,1)S(1)} async-done(((bf16[8,32,1024]{2,1,0:T(8,128)(2,1)}), bf16[8,32,1024]{2,1,0:T(8,128)(2,1)S(1)}, u32[]{:S(2)}, u32[]{:S(2)}) %all-to-all-start.2) | async-done | bytes 524320 | tf_op jit(solution)/shard_map/all_to_all | solution.py:262
  109.8 0.7 reduce_sum.22
  (20 shorter events, 0.1 us)
Async XLA Ops:
  0.6 7.4 %copy-start.4 = (bf16[32,1024]{1,0:T(8,128)(2,1)S(1)}, bf16[32,1024]{1,0:T(8,128)(2,1)}, u32[]{:S(2)}) copy-start(bf16[32,1024]{1,0:T(8,128)(2,1)} %param.7) | copy-start | bytes 196612
  2.4 15.2 %all-to-all-start.1 = ((bf16[8,32,1024]{2,1,0:T(8,128)(2,1)}), bf16[8,32,1024]{2,1,0:T(8,128)(2,1)S(1)}, u32[]{:S(2)}, u32[]{:S(2)}) async-start(bf16[8,32,1024]{2,1,0:T(8,128)(2,1)} %broadcast_in_dim.5), calls=%async_computation.1 | async-start | bytes 1048576 | tf_op jit(solution)/shard_map/all_to_all | solution.py:232
  8.0 4.4 %collective-permute-start = (bf16[32,1024]{1,0:T(8,128)(2,1)S(1)}, bf16[32,1024]{1,0:T(8,128)(2,1)S(1)}, u32[]{:S(2)}, u32[]{:S(2)}) collective-permute-start(bf16[32,1024]{1,0:T(8,128)(2,1)S(1)} %copy-done.4), channel_id=1, source_target_pairs={{0,2},{1,3},{2,0},{3,1},{4,6},{5,7},{6,4},{7,5},{8,10},{9,11},{10,... | collective-permute-start | bytes 196616 | tf_op jit(solution)/shard_map/ppermute | solution.py:227
  18.7 19.0 %copy-start.5 = (s32[64,24]{0,1:T(8,128)S(1)}, s32[64,24]{0,1:T(8,128)}, u32[]{:S(2)}) copy-start(s32[64,24]{0,1:T(8,128)} %param.10) | copy-start | bytes 18436
  18.7 22.9 %copy-start = (bf16[1024,256]{1,0:T(8,128)(2,1)S(1)}, bf16[1024,256]{1,0:T(8,128)(2,1)}, u32[]{:S(2)}) copy-start(bf16[1024,256]{1,0:T(8,128)(2,1)} %q_ref.1) | copy-start | bytes 1572868
  18.7 22.9 %copy-start.1 = (bf16[1024,256]{1,0:T(8,128)(2,1)S(1)}, bf16[1024,256]{1,0:T(8,128)(2,1)}, u32[]{:S(2)}) copy-start(bf16[1024,256]{1,0:T(8,128)(2,1)} %do_ref.1) | copy-start | bytes 1572868
  18.7 22.9 %copy-start.2 = (s32[64]{0:T(128)S(1)}, s32[64]{0:T(128)}, u32[]{:S(2)}) copy-start(s32[64]{0:T(128)} %count_ref.1) | copy-start | bytes 772
  18.7 18.5 %all-to-all-start = ((bf16[8,2,32,1024]{3,2,1,0:T(8,128)(2,1)}), bf16[8,2,32,1024]{3,2,1,0:T(8,128)(2,1)}, u32[]{:S(2)}, u32[]{:S(2)}) async-start(bf16[8,2,32,1024]{3,2,1,0:T(8,128)(2,1)} %broadcast_in_dim.4), calls=%async_computation | async-start | bytes 2097152 | tf_op jit(solution)/shard_map/all_to_all | solution.py:232
  23.1 14.6 %collective-permute-start.2 = (bf16[8,32,1024]{2,1,0:T(8,128)(2,1)S(1)}, bf16[8,32,1024]{2,1,0:T(8,128)(2,1)S(1)}, u32[]{:S(2)}, u32[]{:S(2)}) collective-permute-start(bf16[8,32,1024]{2,1,0:T(8,128)(2,1)S(1)} %all-to-all-done.1.va_ref), channel_id=1, source_target_pairs={{0,2},{1,3},{2,0},{3,1},{4,6},{5,7},{6,4},{7,5},{8,10},{9,11},{10,... | collective-permute-start | bytes 1572872 | tf_op jit(solution)/shard_map/ppermute | solution.py:227
  37.2 4.5 %collective-permute-start.1 = (bf16[8,2,32,1024]{3,2,1,0:T(8,128)(2,1)}, bf16[8,2,32,1024]{3,2,1,0:T(8,128)(2,1)}, u32[]{:S(2)}, u32[]{:S(2)}) collective-permute-start(bf16[8,2,32,1024]{3,2,1,0:T(8,128)(2,1)} %all-to-all-done.ka_ref), channel_id=1, source_target_pairs={{0,1},{1,0},{2,3},{3,2},{4,5},{5,4},{6,7},{7,6},{8,9},{9,8},{10,11... | collective-permute-start | bytes 3145736 | tf_op jit(solution)/shard_map/ppermute | solution.py:227
  37.2 3.0 %collective-permute-start.3 = (bf16[8,32,1024]{2,1,0:T(8,128)(2,1)S(1)}, bf16[8,32,1024]{2,1,0:T(8,128)(2,1)S(1)}, u32[]{:S(2)}, u32[]{:S(2)}) collective-permute-start(bf16[8,32,1024]{2,1,0:T(8,128)(2,1)S(1)} %all-to-all-done.1.va_ref), channel_id=1, source_target_pairs={{0,1},{1,0},{2,3},{3,2},{4,5},{5,4},{6,7},{7,6},{8,9},{9,8},{10,11... | collective-permute-start | bytes 1572872 | tf_op jit(solution)/shard_map/ppermute | solution.py:227
  37.7 3.6 %collective-permute-start.4 = (bf16[8,32,1024]{2,1,0:T(8,128)(2,1)S(1)}, bf16[8,32,1024]{2,1,0:T(8,128)(2,1)S(1)}, u32[]{:S(2)}, u32[]{:S(2)}) collective-permute-start(bf16[8,32,1024]{2,1,0:T(8,128)(2,1)S(1)} %collective-permute-done.2.vb_ref), channel_id=1, source_target_pairs={{0,1},{1,0},{2,3},{3,2},{4,5},{5,4},{6,7},{7,6},{8,9},{9,8},{10,11... | collective-permute-start | bytes 1572872 | tf_op jit(solution)/shard_map/ppermute | solution.py:227
  58.8 3.0 %collective-permute-start.7 = (bf16[8,2,32,1024]{3,2,1,0:T(8,128)(2,1)S(1)}, bf16[8,2,32,1024]{3,2,1,0:T(8,128)(2,1)S(1)}, u32[]{:S(2)}, u32[]{:S(2)}) collective-permute-start(bf16[8,2,32,1024]{3,2,1,0:T(8,128)(2,1)S(1)} %get-tuple-element.17), channel_id=1, source_target_pairs={{0,1},{1,0},{2,3},{3,2},{4,5},{5,4},{6,7},{7,6},{8,9},{9,8},{10,11... | collective-permute-start | bytes 3145736 | tf_op jit(solution)/shard_map/ppermute | solution.py:227
  59.0 21.6 %collective-permute-start.5 = (bf16[8,2,32,1024]{3,2,1,0:T(8,128)(2,1)}, bf16[8,2,32,1024]{3,2,1,0:T(8,128)(2,1)S(1)}, u32[]{:S(2)}, u32[]{:S(2)}) collective-permute-start(bf16[8,2,32,1024]{3,2,1,0:T(8,128)(2,1)} %get-tuple-element.15), channel_id=1, source_target_pairs={{0,1},{1,0},{2,3},{3,2},{4,5},{5,4},{6,7},{7,6},{8,9},{9,8},{10,11... | collective-permute-start | bytes 3145736 | tf_op jit(solution)/shard_map/ppermute | solution.py:227
  63.2 17.5 %copy-start.3 = (bf16[8,2,32,1024]{3,2,1,0:T(8,128)(2,1)S(1)}, bf16[8,2,32,1024]{3,2,1,0:T(8,128)(2,1)}, u32[]{:S(2)}) copy-start(bf16[8,2,32,1024]{3,2,1,0:T(8,128)(2,1)} %get-tuple-element.14) | copy-start | bytes 3145732
  63.2 32.7 %all-to-all-start.3 = ((bf16[8,2,32,1024]{3,2,1,0:T(8,128)(2,1)}), bf16[8,2,32,1024]{3,2,1,0:T(8,128)(2,1)S(1)}, u32[]{:S(2)}, u32[]{:S(2)}) async-start(bf16[8,2,32,1024]{3,2,1,0:T(8,128)(2,1)} %add_convert_fusion), calls=%async_computation.3 | async-start | bytes 2097152 | tf_op jit(solution)/shard_map/all_to_all | solution.py:260
  81.1 13.8 %collective-permute-start.6 = (bf16[8,32,1024]{2,1,0:T(8,128)(2,1)S(1)}, bf16[8,32,1024]{2,1,0:T(8,128)(2,1)S(1)}, u32[]{:S(2)}, u32[]{:S(2)}) collective-permute-start(bf16[8,32,1024]{2,1,0:T(8,128)(2,1)S(1)} %slice_bitcast_fusion), channel_id=1, source_target_pairs={{0,2},{1,3},{2,0},{3,1},{4,6},{5,7},{6,4},{7,5},{8,10},{9,11},{10,... | collective-permute-start | bytes 1572872 | tf_op jit(solution)/shard_map/ppermute | solution.py:227
  95.9 13.9 %all-to-all-start.2 = ((bf16[8,32,1024]{2,1,0:T(8,128)(2,1)}), bf16[8,32,1024]{2,1,0:T(8,128)(2,1)S(1)}, u32[]{:S(2)}, u32[]{:S(2)}) async-start(bf16[8,32,1024]{2,1,0:T(8,128)(2,1)} %fusion), calls=%async_computation.2 | async-start | bytes 1048576 | tf_op jit(solution)/shard_map/all_to_all | solution.py:262
  101.5 5.1 %collective-permute-start.8 = (f32[32,1024]{1,0:T(8,128)S(1)}, f32[32,1024]{1,0:T(8,128)S(1)}, u32[]{:S(2)}, u32[]{:S(2)}) collective-permute-start(f32[32,1024]{1,0:T(8,128)S(1)} %slice_bitcast_fusion.2), channel_id=1, source_target_pairs={{0,2},{1,3},{2,0},{3,1},{4,6},{5,7},{6,4},{7,5},{8,10},{9,11},{10,... | collective-permute-start | bytes 393224 | tf_op jit(solution)/shard_map/ppermute | solution.py:227

commit v5 on v4

--- a/solution.py
+++ b/solution.py
@@ -254,9 +254,11 @@
     def add(left, right):
         return left.astype(jnp.float32) + right.astype(jnp.float32)
 
-    v_half = add(v_keep, swap(v_send, 1)).astype(jnp.bfloat16)
+    v_got_half = swap(v_send, 1)
+    v_away = add(v_keep[:, 1], v_got_half[:, 1]).astype(jnp.bfloat16)
     k_half = add(k_keep, swap(k_send, 1)).astype(jnp.bfloat16)
-    v_quarter = add(v_half[:, 0], swap(v_half[:, 1], 2)).astype(jnp.bfloat16)
+    v_mine_sum = add(v_keep[:, 0], v_got_half[:, 0])
+    v_quarter = add(v_mine_sum, swap(v_away, 2)).astype(jnp.bfloat16)
     k_got = lax.all_to_all(k_half, "seq", 0, 0)
     k_sum = jnp.sum(k_got.astype(jnp.float32), axis=0)
     v_got = lax.all_to_all(v_quarter, "seq", 0, 0)

time: 111 us -> 112 us (level); the launches traced: 111 us -> 113 us
  starting transfers between devices: 36.2 us -> 37.7 us
    all_to_all x1, starting transfers between devices: 17.5 us -> 19.2 us  [per_device(): k_got = lax.all_to_all(k_half, 'seq', 0, 0)]
where the time goes in v5:
time: 112 us; the launch traced here: 113 us
  waiting for transfers between devices  49.3 us (44%)
  starting transfers between devices  37.7 us (34%)
  Pallas kernels  17.7 us (16%)
  other arithmetic  4.3 us (4%)
  local copies, waits for them, and re-layouts  2.96 us (3%)
    ppermute x9, waiting for transfers between devices, swap(): lax.ppermute(value, 'head', [(i, i ^ bit) for i in range(lax.axis_size('h...  27.9 us
    all_to_all x1, starting transfers between devices, per_device(): k_got = lax.all_to_all(k_half, 'seq', 0, 0)  19.2 us
    all_to_all x2, waiting for transfers between devices, send_all(): lax.all_to_all(jnp.broadcast_to(value[None], (shards,) + value.shape), 's...  18.7 us
    pallas_call x1, Pallas kernels, attend(): pl.pallas_call(attend_kernel, in_specs=[scalar] * 3 + [whole] * 2 + [away...  17.7 us
    all_to_all x2, starting transfers between devices, send_all(): lax.all_to_all(jnp.broadcast_to(value[None], (shards,) + value.shape), 's...  10.1 us
    all_to_all x1, starting transfers between devices, per_device(): v_got = lax.all_to_all(v_quarter, 'seq', 0, 0)  5.41 us
    ppermute x9, starting transfers between devices, swap(): lax.ppermute(value, 'head', [(i, i ^ bit) for i in range(lax.axis_size('h...  3.09 us
    broadcast_in_dim x2, local copies, waits for them, and re-layouts, send_all(): jnp.broadcast_to(value[None], (shards,) + value.shape)  2.85 us
  transfers between devices with their start and end apart: 13, of which 10 were waited for; matrix products, arithmetic and copies ran while one was open for 3% of the time, Pallas kernels for 0%

profile of v5, /device:TPU:8, one launch (start us, length us, event | category | flops | bytes accessed | tf_op | source)
XLA Modules:
  0.0 112.7 jit_solution(5681937818545617367)
XLA Ops:
  0.6 1.7 %broadcast_in_dim.5 = bf16[8,32,1024]{2,1,0:T(8,128)(2,1)} broadcast(bf16[32,1024]{1,0:T(8,128)(2,1)} %param.8), dimensions={1,2} | broadcast | bytes 589824 | tf_op jit(solution)/shard_map/broadcast_in_dim | solution.py:232
  2.4 5.7 %all-to-all-start.1 = ((bf16[8,32,1024]{2,1,0:T(8,128)(2,1)}), bf16[8,32,1024]{2,1,0:T(8,128)(2,1)S(1)}, u32[]{:S(2)}, u32[]{:S(2)}) async-start(bf16[8,32,1024]{2,1,0:T(8,128)(2,1)} %broadcast_in_dim.5), calls=%async_computation.1 | async-start | bytes 1048576 | tf_op jit(solution)/shard_map/all_to_all | solution.py:232
  8.0 0.5 collective-permute-start
  8.6 3.8 %collective-permute-done = bf16[32,1024]{1,0:T(8,128)(2,1)S(1)} collective-permute-done((bf16[32,1024]{1,0:T(8,128)(2,1)S(1)}, bf16[32,1024]{1,0:T(8,128)(2,1)S(1)}, u32[]{:S(2)}, u32[]{:S(2)}) %collective-permute-start) | collective-permute-done | bytes 65568 | tf_op jit(solution)/shard_map/ppermute | solution.py:227
  12.4 5.2 %all-to-all-done.1.va_ref = bf16[8,32,1024]{2,1,0:T(8,128)(2,1)S(1)} async-done(((bf16[8,32,1024]{2,1,0:T(8,128)(2,1)}), bf16[8,32,1024]{2,1,0:T(8,128)(2,1)S(1)}, u32[]{:S(2)}, u32[]{:S(2)}) %all-to-all-start.1) | async-done | bytes 524320 | tf_op jit(solution)/shard_map/all_to_all | solution.py:232
  17.6 1.1 broadcast_in_dim.4
  18.7 4.4 %all-to-all-start = ((bf16[8,2,32,1024]{3,2,1,0:T(8,128)(2,1)}), bf16[8,2,32,1024]{3,2,1,0:T(8,128)(2,1)}, u32[]{:S(2)}, u32[]{:S(2)}) async-start(bf16[8,2,32,1024]{3,2,1,0:T(8,128)(2,1)} %broadcast_in_dim.4), calls=%async_computation | async-start | bytes 2097152 | tf_op jit(solution)/shard_map/all_to_all | solution.py:232
  23.1 0.5 collective-permute-start.2
  23.7 13.5 %all-to-all-done.ka_ref = bf16[8,2,32,1024]{3,2,1,0:T(8,128)(2,1)} async-done(((bf16[8,2,32,1024]{3,2,1,0:T(8,128)(2,1)}), bf16[8,2,32,1024]{3,2,1,0:T(8,128)(2,1)}, u32[]{:S(2)}, u32[]{:S(2)}) %all-to-all-start) | async-done | bytes 1048608 | tf_op jit(solution)/shard_map/all_to_all | solution.py:232
  37.2 0.5 collective-permute-start.3
  37.7 0.1 copy.10.blocks_ref
  37.8 0.1 pad_add_fusion.where_ref
  37.9 2.4 %collective-permute-done.3.vc_ref = bf16[8,32,1024]{2,1,0:T(8,128)(2,1)S(1)} collective-permute-done((bf16[8,32,1024]{2,1,0:T(8,128)(2,1)S(1)}, bf16[8,32,1024]{2,1,0:T(8,128)(2,1)S(1)}, u32[]{:S(2)}, u32[]{:S(2)}) %collective-permute-start.3) | collective-permute-done | bytes 524320 | tf_op jit(solution)/shard_map/ppermute | solution.py:227
  40.2 1.1 collective-permute-done.4.vd_ref
  41.4 0.3 collective-permute-done.1.kc_ref
  41.7 17.7 %attend.1 = (bf16[1024,256]{1,0:T(8,128)(2,1)}, bf16[1024,256]{1,0:T(8,128)(2,1)}, bf16[8,2,32,1024]{3,2,1,0:T(8,128)(2,1)S(1)}, bf16[8,2,32,1024]{3,2,1,0:T(8,1...) custom-call(s32[2]{0:T(128)S(1)} %pad_add_fusion.where_ref, ...), custom_call_target="tpu_custom_call" | custom-call | tf_op jit(solution)/shard_map/attend/pallas_call | solution.py:205
  59.4 0.2 collective-permute-start.7
  59.6 0.4 collective-permute-start.5
  59.9 2.4 %collective-permute-done.7 = bf16[8,2,32,1024]{3,2,1,0:T(8,128)(2,1)S(1)} collective-permute-done((bf16[8,2,32,1024]{3,2,1,0:T(8,128)(2,1)S(1)}, bf16[8,2,32,1024]{3,2,1,0:T(8,128)(2,1)S(1)}, u32[]{:S(2)}, u32[]{:S(2)}) %collective-permute-start.7) | collective-permute-done | bytes 1048608 | tf_op jit(solution)/shard_map/ppermute | solution.py:227
  62.4 1.4 %add_convert_fusion = bf16[8,2,32,1024]{3,2,1,0:T(8,128)(2,1)} fusion(bf16[8,2,32,1024]{3,2,1,0:T(8,128)(2,1)S(1)} %collective-permute-done.7, bf16[8,2,32,1024]{3,2,1,0:T(8,128)(2,1)S(1)} %get-tuple-element.16), kind=kLoop, calls=%fused_computation.1 | loop fusion | flops 2097152 | bytes 3145728 | tf_op jit(solution)/shard_map/convert_element_type | solution.py:259
  63.8 19.2 %all-to-all-start.3 = ((bf16[8,2,32,1024]{3,2,1,0:T(8,128)(2,1)}), bf16[8,2,32,1024]{3,2,1,0:T(8,128)(2,1)S(1)}, u32[]{:S(2)}, u32[]{:S(2)}) async-start(bf16[8,2,32,1024]{3,2,1,0:T(8,128)(2,1)} %add_convert_fusion), calls=%async_computation.3 | async-start | bytes 2097152 | tf_op jit(solution)/shard_map/all_to_all | solution.py:262
  83.0 0.2 fusion.1
  83.2 0.5 collective-permute-start.6
  83.6 13.3 %collective-permute-done.6 = bf16[8,32,1024]{2,1,0:T(8,128)(2,1)S(1)} collective-permute-done((bf16[8,32,1024]{2,1,0:T(8,128)(2,1)S(1)}, bf16[8,32,1024]{2,1,0:T(8,128)(2,1)S(1)}, u32[]{:S(2)}, u32[]{:S(2)}) %collective-permute-start.6) | collective-permute-done | bytes 524320 | tf_op jit(solution)/shard_map/ppermute | solution.py:227
  96.9 1.1 fusion
  98.1 5.4 %all-to-all-start.2 = ((bf16[8,32,1024]{2,1,0:T(8,128)(2,1)}), bf16[8,32,1024]{2,1,0:T(8,128)(2,1)S(1)}, u32[]{:S(2)}, u32[]{:S(2)}) async-start(bf16[8,32,1024]{2,1,0:T(8,128)(2,1)} %fusion), calls=%async_computation.2 | async-start | bytes 1048576 | tf_op jit(solution)/shard_map/all_to_all | solution.py:264
  103.5 0.2 convert_reduce_fusion
  103.7 0.5 collective-permute-start.8
  104.1 4.6 %collective-permute-done.8 = f32[32,1024]{1,0:T(8,128)S(1)} collective-permute-done((f32[32,1024]{1,0:T(8,128)S(1)}, f32[32,1024]{1,0:T(8,128)S(1)}, u32[]{:S(2)}, u32[]{:S(2)}) %collective-permute-start.8) | collective-permute-done | bytes 131104 | tf_op jit(solution)/shard_map/ppermute | solution.py:227
  108.7 0.6 fusion.3
  109.4 2.6 %all-to-all-done.2 = bf16[8,32,1024]{2,1,0:T(8,128)(2,1)S(1)} async-done(((bf16[8,32,1024]{2,1,0:T(8,128)(2,1)}), bf16[8,32,1024]{2,1,0:T(8,128)(2,1)S(1)}, u32[]{:S(2)}, u32[]{:S(2)}) %all-to-all-start.2) | async-done | bytes 524320 | tf_op jit(solution)/shard_map/all_to_all | solution.py:264
  112.0 0.7 reduce_sum.22
  (19 shorter events, 0.1 us)
Async XLA Ops:
  0.6 7.4 %copy-start.4 = (bf16[32,1024]{1,0:T(8,128)(2,1)S(1)}, bf16[32,1024]{1,0:T(8,128)(2,1)}, u32[]{:S(2)}) copy-start(bf16[32,1024]{1,0:T(8,128)(2,1)} %param.7) | copy-start | bytes 196612
  2.4 15.2 %all-to-all-start.1 = ((bf16[8,32,1024]{2,1,0:T(8,128)(2,1)}), bf16[8,32,1024]{2,1,0:T(8,128)(2,1)S(1)}, u32[]{:S(2)}, u32[]{:S(2)}) async-start(bf16[8,32,1024]{2,1,0:T(8,128)(2,1)} %broadcast_in_dim.5), calls=%async_computation.1 | async-start | bytes 1048576 | tf_op jit(solution)/shard_map/all_to_all | solution.py:232
  8.0 4.4 %collective-permute-start = (bf16[32,1024]{1,0:T(8,128)(2,1)S(1)}, bf16[32,1024]{1,0:T(8,128)(2,1)S(1)}, u32[]{:S(2)}, u32[]{:S(2)}) collective-permute-start(bf16[32,1024]{1,0:T(8,128)(2,1)S(1)} %copy-done.4), channel_id=1, source_target_pairs={{0,2},{1,3},{2,0},{3,1},{4,6},{5,7},{6,4},{7,5},{8,10},{9,11},{10,... | collective-permute-start | bytes 196616 | tf_op jit(solution)/shard_map/ppermute | solution.py:227
  18.7 19.0 %copy-start.5 = (s32[64,24]{0,1:T(8,128)S(1)}, s32[64,24]{0,1:T(8,128)}, u32[]{:S(2)}) copy-start(s32[64,24]{0,1:T(8,128)} %param.10) | copy-start | bytes 18436
  18.7 22.9 %copy-start = (bf16[1024,256]{1,0:T(8,128)(2,1)S(1)}, bf16[1024,256]{1,0:T(8,128)(2,1)}, u32[]{:S(2)}) copy-start(bf16[1024,256]{1,0:T(8,128)(2,1)} %q_ref.1) | copy-start | bytes 1572868
  18.7 22.9 %copy-start.1 = (bf16[1024,256]{1,0:T(8,128)(2,1)S(1)}, bf16[1024,256]{1,0:T(8,128)(2,1)}, u32[]{:S(2)}) copy-start(bf16[1024,256]{1,0:T(8,128)(2,1)} %do_ref.1) | copy-start | bytes 1572868
  18.7 22.9 %copy-start.2 = (s32[64]{0:T(128)S(1)}, s32[64]{0:T(128)}, u32[]{:S(2)}) copy-start(s32[64]{0:T(128)} %count_ref.1) | copy-start | bytes 772
  18.7 18.5 %all-to-all-start = ((bf16[8,2,32,1024]{3,2,1,0:T(8,128)(2,1)}), bf16[8,2,32,1024]{3,2,1,0:T(8,128)(2,1)}, u32[]{:S(2)}, u32[]{:S(2)}) async-start(bf16[8,2,32,1024]{3,2,1,0:T(8,128)(2,1)} %broadcast_in_dim.4), calls=%async_computation | async-start | bytes 2097152 | tf_op jit(solution)/shard_map/all_to_all | solution.py:232
  23.1 14.6 %collective-permute-start.2 = (bf16[8,32,1024]{2,1,0:T(8,128)(2,1)S(1)}, bf16[8,32,1024]{2,1,0:T(8,128)(2,1)S(1)}, u32[]{:S(2)}, u32[]{:S(2)}) collective-permute-start(bf16[8,32,1024]{2,1,0:T(8,128)(2,1)S(1)} %all-to-all-done.1.va_ref), channel_id=1, source_target_pairs={{0,2},{1,3},{2,0},{3,1},{4,6},{5,7},{6,4},{7,5},{8,10},{9,11},{10,... | collective-permute-start | bytes 1572872 | tf_op jit(solution)/shard_map/ppermute | solution.py:227
  37.2 4.5 %collective-permute-start.1 = (bf16[8,2,32,1024]{3,2,1,0:T(8,128)(2,1)}, bf16[8,2,32,1024]{3,2,1,0:T(8,128)(2,1)}, u32[]{:S(2)}, u32[]{:S(2)}) collective-permute-start(bf16[8,2,32,1024]{3,2,1,0:T(8,128)(2,1)} %all-to-all-done.ka_ref), channel_id=1, source_target_pairs={{0,1},{1,0},{2,3},{3,2},{4,5},{5,4},{6,7},{7,6},{8,9},{9,8},{10,11... | collective-permute-start | bytes 3145736 | tf_op jit(solution)/shard_map/ppermute | solution.py:227
  37.2 3.0 %collective-permute-start.3 = (bf16[8,32,1024]{2,1,0:T(8,128)(2,1)S(1)}, bf16[8,32,1024]{2,1,0:T(8,128)(2,1)S(1)}, u32[]{:S(2)}, u32[]{:S(2)}) collective-permute-start(bf16[8,32,1024]{2,1,0:T(8,128)(2,1)S(1)} %all-to-all-done.1.va_ref), channel_id=1, source_target_pairs={{0,1},{1,0},{2,3},{3,2},{4,5},{5,4},{6,7},{7,6},{8,9},{9,8},{10,11... | collective-permute-start | bytes 1572872 | tf_op jit(solution)/shard_map/ppermute | solution.py:227
  37.7 3.6 %collective-permute-start.4 = (bf16[8,32,1024]{2,1,0:T(8,128)(2,1)S(1)}, bf16[8,32,1024]{2,1,0:T(8,128)(2,1)S(1)}, u32[]{:S(2)}, u32[]{:S(2)}) collective-permute-start(bf16[8,32,1024]{2,1,0:T(8,128)(2,1)S(1)} %collective-permute-done.2.vb_ref), channel_id=1, source_target_pairs={{0,1},{1,0},{2,3},{3,2},{4,5},{5,4},{6,7},{7,6},{8,9},{9,8},{10,11... | collective-permute-start | bytes 1572872 | tf_op jit(solution)/shard_map/ppermute | solution.py:227
  59.4 3.0 %collective-permute-start.7 = (bf16[8,2,32,1024]{3,2,1,0:T(8,128)(2,1)S(1)}, bf16[8,2,32,1024]{3,2,1,0:T(8,128)(2,1)S(1)}, u32[]{:S(2)}, u32[]{:S(2)}) collective-permute-start(bf16[8,2,32,1024]{3,2,1,0:T(8,128)(2,1)S(1)} %get-tuple-element.17), channel_id=1, source_target_pairs={{0,1},{1,0},{2,3},{3,2},{4,5},{5,4},{6,7},{7,6},{8,9},{9,8},{10,11... | collective-permute-start | bytes 3145736 | tf_op jit(solution)/shard_map/ppermute | solution.py:227
  59.6 23.4 %collective-permute-start.5 = (bf16[8,2,32,1024]{3,2,1,0:T(8,128)(2,1)}, bf16[8,2,32,1024]{3,2,1,0:T(8,128)(2,1)S(1)}, u32[]{:S(2)}, u32[]{:S(2)}) collective-permute-start(bf16[8,2,32,1024]{3,2,1,0:T(8,128)(2,1)} %get-tuple-element.15), channel_id=1, source_target_pairs={{0,1},{1,0},{2,3},{3,2},{4,5},{5,4},{6,7},{7,6},{8,9},{9,8},{10,11... | collective-permute-start | bytes 3145736 | tf_op jit(solution)/shard_map/ppermute | solution.py:227
  63.8 19.2 %copy-start.3 = (bf16[8,2,32,1024]{3,2,1,0:T(8,128)(2,1)S(1)}, bf16[8,2,32,1024]{3,2,1,0:T(8,128)(2,1)}, u32[]{:S(2)}) copy-start(bf16[8,2,32,1024]{3,2,1,0:T(8,128)(2,1)} %get-tuple-element.14) | copy-start | bytes 3145732
  63.8 34.3 %all-to-all-start.3 = ((bf16[8,2,32,1024]{3,2,1,0:T(8,128)(2,1)}), bf16[8,2,32,1024]{3,2,1,0:T(8,128)(2,1)S(1)}, u32[]{:S(2)}, u32[]{:S(2)}) async-start(bf16[8,2,32,1024]{3,2,1,0:T(8,128)(2,1)} %add_convert_fusion), calls=%async_computation.3 | async-start | bytes 2097152 | tf_op jit(solution)/shard_map/all_to_all | solution.py:262
  83.2 13.8 %collective-permute-start.6 = (bf16[8,32,1024]{2,1,0:T(8,128)(2,1)S(1)}, bf16[8,32,1024]{2,1,0:T(8,128)(2,1)S(1)}, u32[]{:S(2)}, u32[]{:S(2)}) collective-permute-start(bf16[8,32,1024]{2,1,0:T(8,128)(2,1)S(1)} %fusion.1), channel_id=1, source_target_pairs={{0,2},{1,3},{2,0},{3,1},{4,6},{5,7},{6,4},{7,5},{8,10},{9,11},{10,... | collective-permute-start | bytes 1572872 | tf_op jit(solution)/shard_map/ppermute | solution.py:227
  98.1 13.9 %all-to-all-start.2 = ((bf16[8,32,1024]{2,1,0:T(8,128)(2,1)}), bf16[8,32,1024]{2,1,0:T(8,128)(2,1)S(1)}, u32[]{:S(2)}, u32[]{:S(2)}) async-start(bf16[8,32,1024]{2,1,0:T(8,128)(2,1)} %fusion), calls=%async_computation.2 | async-start | bytes 1048576 | tf_op jit(solution)/shard_map/all_to_all | solution.py:264
  103.7 5.1 %collective-permute-start.8 = (f32[32,1024]{1,0:T(8,128)S(1)}, f32[32,1024]{1,0:T(8,128)S(1)}, u32[]{:S(2)}, u32[]{:S(2)}) collective-permute-start(f32[32,1024]{1,0:T(8,128)S(1)} %slice_bitcast_fusion.1), channel_id=1, source_target_pairs={{0,2},{1,3},{2,0},{3,1},{4,6},{5,7},{6,4},{7,5},{8,10},{9,11},{10,... | collective-permute-start | bytes 393224 | tf_op jit(solution)/shard_map/ppermute | solution.py:227
